TPU v7x, 32 devices: a whole 2x2x4 slice. The times are simulated.
32 devices in a mesh: group: 2 (over x), chan: 16 (over z, y, core).
Axes of the slice: x: 2, y: 2, z: 4, core: 2. Of those that a mesh axis runs over, the one named last changes fastest.
Arguments:
- voltages: bfloat16 [32, 2, 256, 1024], P(('group', 'chan')), parts along dimension 0, may hold values from -6 to 6
- cal_num: float32 [32, 4, 512], P(('group', 'chan')), parts along dimension 0, may hold values from -6 to 6
- cal_weight: float32 [32, 2, 512], P(('group', 'chan')), parts along dimension 0, may hold values from 0.2 to 5
- flags: int32 [32, 512], P(('group', 'chan')), parts along dimension 0, may hold values 0 or 1
- positions: float32 [2, 512], replicated, may hold values from -300 to 300
- directions: float32 [2, 1024], replicated, may hold values from -0.05 to 0.05
- pointing: int32 [2048], P('group'), parts along dimension 0, may hold values from 0 to 1023, each once
Outputs:
- beam_power: bfloat16 [2048, 16, 128], P(('group', 'chan')), parts along dimension 0
- solved_gains: float32 [32, 4, 512], P(('group', 'chan')), parts along dimension 0
There are 2 independent parts, one for each index of `group`. A program takes and returns all parts, laid end to end along the dimension named above; an argument that names none is the same for every part. Nothing has to cross between parts.
Inputs may be any that keep to these rules, and one draw needn't show every extreme that they name: `pointing`: each table direction is named by exactly one beam.
All inputs are finite; a program needn't handle non-finite values. No bound on the sum of `flags` on one device may be relied on, other than what follows from the above.
Results may differ from a plain program's by a relative error of at most 0.004.
Values may be sent and summed in bfloat16 or wider, within the bound.
No kernel may reach another device: no remote copies, remote signals or barrier semaphores. Data moves between devices by JAX's collectives and lax.ppermute only.
A program may use at most 64 MiB of HBM per device.

v0:
```python
import jax
import jax.numpy as jnp
from jax import lax
from jax.sharding import PartitionSpec as P

ITERS = 8


PENALTY = 2.0
RIDGE = 1.0
TWO_PI = 6.283185307179586
HIGHEST = lax.Precision.HIGHEST


def basis_rows(channel_ids, total):
    place = 2.0 * (channel_ids.astype(jnp.float32) + 0.5) / total - 1.0
    return jnp.stack(
        [
            jnp.ones_like(place),
            place,
            0.5 * (3.0 * place * place - 1.0),
            0.5 * (5.0 * place * place * place - 3.0 * place),
        ],
        axis=1,
    )


def invert_small(matrix):
    order = matrix.shape[0]
    unit = jnp.ones_like(matrix[0, 0])
    nothing = jnp.zeros_like(matrix[0, 0])
    left = [[matrix[row, column] for column in range(order)] for row in range(order)]
    right = [
        [unit if row == column else nothing for column in range(order)] for row in range(order)
    ]
    for pivot in range(order):
        factor = 1.0 / left[pivot][pivot]
        left[pivot] = [entry * factor for entry in left[pivot]]
        right[pivot] = [entry * factor for entry in right[pivot]]
        for row in range(order):
            if row != pivot:
                scale = left[row][pivot]
                left[row] = [
                    first - scale * second for first, second in zip(left[row], left[pivot])
                ]
                right[row] = [
                    first - scale * second for first, second in zip(right[row], right[pivot])
                ]
    return jnp.stack([jnp.stack(line, 0) for line in right], 0)


def beam_matrices(fitted, usable, ratio, projected):
    phase = projected * (TWO_PI * ratio)
    cosine = jnp.cos(phase)
    sine = jnp.sin(phase)
    stations = projected.shape[1]
    scale = usable * stations ** (-0.5)
    matrices = []
    for polar in range(2):
        gain_re = (fitted[2 * polar] * scale)[None, :]
        gain_im = (fitted[2 * polar + 1] * scale)[None, :]
        w_re = (gain_re * cosine - gain_im * sine).astype(jnp.bfloat16)
        w_im = (-(gain_re * sine + gain_im * cosine)).astype(jnp.bfloat16)
        upper = jnp.concatenate([w_re, -w_im], axis=1)
        lower = jnp.concatenate([w_im, w_re], axis=1)
        matrices.append(jnp.concatenate([upper, lower], axis=0))
    return matrices


def detect(matrices, volts):
    beams = matrices[0].shape[0] // 2
    total = jnp.zeros((beams, volts.shape[1]), jnp.float32)
    for polar in range(2):
        output = lax.dot_general(
            matrices[polar],
            volts[polar],
            (((1,), (1,)), ((), ())),
            preferred_element_type=jnp.float32,
        )
        total = total + output[:beams] * output[:beams] + output[beams:] * output[beams:]
    return total


def average_pairs(power):
    return ((power[..., 0::2] + power[..., 1::2]) * 0.5).astype(jnp.bfloat16)


def body(voltages, cal_num, cal_weight, flags, positions, directions, pointing):
    local_count = voltages.shape[0]
    devices = lax.axis_size("chan")
    total = local_count * devices
    channel_ids = lax.axis_index("chan") * local_count + jnp.arange(local_count, dtype=jnp.int32)
    basis = basis_rows(channel_ids, total)
    usable = flags.astype(jnp.float32)
    gram = jnp.einsum("ck,cj,cs->kjs", basis, basis, usable, precision=HIGHEST)
    order = basis.shape[1]
    identity = jnp.eye(order, dtype=jnp.float32)[:, :, None]
    weight4 = jnp.repeat(cal_weight, 2, axis=1)
    mask = usable[:, None, :]
    fitted = jnp.zeros(cal_num.shape, jnp.float32)
    dual = jnp.zeros(cal_num.shape, jnp.float32)
    inverse = None
    for sweep in range(ITERS):
        local = (mask * cal_num + PENALTY * (fitted - dual)) / (mask * weight4 + PENALTY)
        numerator = jnp.einsum("ck,cqs->kqs", basis, mask * (local + dual), precision=HIGHEST)
        if sweep == 0:
            gram_all, summed = lax.psum((gram, numerator), "chan")
            inverse = invert_small(gram_all + RIDGE * identity)
        else:
            summed = lax.psum(numerator, "chan")
        coefficients = jnp.einsum("kjs,jqs->kqs", inverse, summed, precision=HIGHEST)
        fitted = jnp.einsum("ck,kqs->cqs", basis, coefficients, precision=HIGHEST)
        dual = dual + mask * (local - fitted)
    table_size = directions.shape[1]
    one_hot = (pointing[:, None] == jnp.arange(table_size, dtype=jnp.int32)[None, :]).astype(
        jnp.float32
    )
    pointed = jnp.dot(one_hot, directions.T, precision=HIGHEST)
    projected = pointed[:, 0:1] * positions[0][None, :] + pointed[:, 1:2] * positions[1][None, :]
    ratio = 1.0 + 0.3 * (channel_ids.astype(jnp.float32) + 0.5) / total
    weights = beam_matrices(fitted[0], usable[0], ratio[0], projected)
    samples = voltages.shape[2]
    half = samples // 2
    pieces = []
    for part_index in range(2):
        start = part_index * half
        powers = [detect(weights, voltages[0, :, start : start + half])]
        pieces.append(
            lax.all_to_all(
                average_pairs(jnp.stack(powers, axis=1)),
                "chan",
                split_axis=0,
                concat_axis=1,
                tiled=True,
            )
        )
    beam_power = jnp.concatenate(pieces, axis=2)
    return (beam_power, fitted)


def solution(mesh):
    return jax.shard_map(
        body,
        mesh=mesh,
        in_specs=(
            P(("group", "chan"), None, None, None),
            P(("group", "chan"), None, None),
            P(("group", "chan"), None, None),
            P(("group", "chan"), None),
            P(),
            P(),
            P("group"),
        ),
        out_specs=(P(("group", "chan"), None, None), P(("group", "chan"), None, None)),
        check_vma=False,
    )
```

profile of v0, /device:TPU:0, one launch (start us, length us, event | category | flops | bytes accessed | tf_op | source)
XLA Modules:
  0.0 697.4 jit_solution(10860283058843665609)
XLA Ops:
  7.4 0.7 convert_element_type.35
  8.1 0.7 broadcast_in_dim.6
  8.8 0.7 multiply_bitcast_fusion
  9.5 0.7 multiply_bitcast_fusion.8
  10.4 1.6 broadcast_multiply_fusion.7
  12.1 2.0 fusion
  14.2 94.6 %all-reduce.3.cloned.1.call-done = (f32[4,4,512]{0,1,2:T(4,128)}, f32[4,4,512]{2,1,0:T(4,128)}) async-done(((f32[4,4,512]{0,1,2:T(4,128)}, f32[4,4,512]{2,1,0:T(4,128)}), (f32[4,4,512]{0,1,2:T(4,128)}, f32[4,4,512]{2,1,0:T(4,128)})) %all-reduce.3.cloned.1.call-update) | async-done | bytes 65552 | tf_op jit(solution)/shard_map/psum | solution.py:107
  108.7 0.9 broadcast_add_fusion
  109.9 0.4 copy.83
  110.4 3.5 convolution_bitcast_fusion.7
  113.9 0.9 fusion.22
  115.1 0.6 broadcast_multiply_fusion.6
  115.7 70.4 %psum.65 = f32[4,4,512]{0,1,2:T(4,128)S(1)} all-reduce(f32[4,4,512]{0,1,2:T(4,128)S(1)} %broadcast_multiply_fusion.6), channel_id=1, replica_groups=mesh['group'=2,'chan'=16] {'chan'}, use_global_device_ids=true, to_apply=%region_2.0 | all-reduce | flops 8192 | bytes 65536 | tf_op jit(solution)/shard_map/psum | solution.py:110
  186.1 3.5 convolution_bitcast_fusion.6
  189.7 0.9 fusion.20
  190.8 0.6 broadcast_multiply_fusion.5
  191.4 69.2 %psum.66 = f32[4,4,512]{0,1,2:T(4,128)S(1)} all-reduce(f32[4,4,512]{0,1,2:T(4,128)S(1)} %broadcast_multiply_fusion.5), channel_id=1, replica_groups=mesh['group'=2,'chan'=16] {'chan'}, use_global_device_ids=true, to_apply=%region_3.0 | all-reduce | flops 8192 | bytes 65536 | tf_op jit(solution)/shard_map/psum | solution.py:110
  260.6 3.5 convolution_bitcast_fusion.5
  264.2 0.9 fusion.18
  265.3 0.6 broadcast_multiply_fusion.4
  265.9 69.3 %psum.67 = f32[4,4,512]{0,1,2:T(4,128)S(1)} all-reduce(f32[4,4,512]{0,1,2:T(4,128)S(1)} %broadcast_multiply_fusion.4), channel_id=1, replica_groups=mesh['group'=2,'chan'=16] {'chan'}, use_global_device_ids=true, to_apply=%region_4.0 | all-reduce | flops 8192 | bytes 65536 | tf_op jit(solution)/shard_map/psum | solution.py:110
  335.3 3.5 convolution_bitcast_fusion.4
  338.9 0.9 fusion.16
  340.0 0.6 broadcast_multiply_fusion.3
  340.6 69.2 %psum.68 = f32[4,4,512]{0,1,2:T(4,128)S(1)} all-reduce(f32[4,4,512]{0,1,2:T(4,128)S(1)} %broadcast_multiply_fusion.3), channel_id=1, replica_groups=mesh['group'=2,'chan'=16] {'chan'}, use_global_device_ids=true, to_apply=%region_5.0 | all-reduce | flops 8192 | bytes 65536 | tf_op jit(solution)/shard_map/psum | solution.py:110
  409.8 3.5 convolution_bitcast_fusion.3
  413.4 0.9 fusion.14
  414.5 0.6 broadcast_multiply_fusion.2
  415.1 69.4 %psum.69 = f32[4,4,512]{0,1,2:T(4,128)S(1)} all-reduce(f32[4,4,512]{0,1,2:T(4,128)S(1)} %broadcast_multiply_fusion.2), channel_id=1, replica_groups=mesh['group'=2,'chan'=16] {'chan'}, use_global_device_ids=true, to_apply=%region_6.0 | all-reduce | flops 8192 | bytes 65536 | tf_op jit(solution)/shard_map/psum | solution.py:110
  484.5 3.5 convolution_bitcast_fusion.2
  488.1 0.9 fusion.12
  489.2 0.6 broadcast_multiply_fusion.1
  489.8 69.2 %psum.70 = f32[4,4,512]{0,1,2:T(4,128)S(1)} all-reduce(f32[4,4,512]{0,1,2:T(4,128)S(1)} %broadcast_multiply_fusion.1), channel_id=1, replica_groups=mesh['group'=2,'chan'=16] {'chan'}, use_global_device_ids=true, to_apply=%region_7.0 | all-reduce | flops 8192 | bytes 65536 | tf_op jit(solution)/shard_map/psum | solution.py:110
  559.0 3.5 convolution_bitcast_fusion.1
  562.6 0.9 fusion.10
  563.7 0.6 broadcast_multiply_fusion
  564.3 69.6 %psum.71 = f32[4,4,512]{0,1,2:T(4,128)S(1)} all-reduce(f32[4,4,512]{0,1,2:T(4,128)S(1)} %broadcast_multiply_fusion), channel_id=1, replica_groups=mesh['group'=2,'chan'=16] {'chan'}, use_global_device_ids=true, to_apply=%region_8.0 | all-reduce | flops 8192 | bytes 65536 | tf_op jit(solution)/shard_map/psum | solution.py:110
  633.9 3.5 convolution_bitcast_fusion
  637.5 0.9 fusion.8
  638.5 8.8 %fusion.80 = (bf16[1024,512]{1,0:T(8,128)(2,1)S(1)}, bf16[1024,512]{1,0:T(8,128)(2,1)S(1)}) fusion(f32[512]{0:T(512)S(1)} %bitcast.311, f32[]{:T(128)S(6)} %mul_shard_map.8, f32[512]{0:T(512)S(1)} %bitcast.315, f32[1024]{0:T(1024)S(1)} %bitcast.302, f32[512]{0:T(512)S(1)} %bitcast.313, f32[1024]{0:T(1024)S(1)} %bitcast.300, f32[512]{0:T(512)S(1)} %bitcast.305, ...), kind=kLoop, calls=%fused_computation.196 | loop fusion | flops 10485760 | bytes 2117636 | tf_op jit(solution)/shard_map/neg | solution.py:64
  647.3 9.3 %negate_convert_fusion.1 = (bf16[1024,512]{1,0:T(8,128)(2,1)S(1)}, bf16[1024,512]{1,0:T(8,128)(2,1)S(1)}, bf16[1024,512]{1,0:T(8,128)(2,1)S(1)}, bf16[1024,512]{1,0:T(8,128)(2,1)S(1)}) fusion(f32[]{:T(128)S(6)} %mul_shard_map.8, f32[512]{0:T(512)S(1)} %bitcast.312, f32[512]{0:T(512)S(1)} %bitcast.316, f32[1024]{0:T(1024)S(1)} %bitcast.303, ...), kind=kLoop, calls=%fused_computation.6 | loop fusion | flops 11534336 | bytes 4214788 | tf_op jit(solution)/shard_map/convert_element_type | solution.py:63
  656.6 1.5 fusion.7
  658.1 1.5 fusion.6
  659.6 1.5 fusion.4
  661.1 1.5 fusion.5
  662.6 0.2 fusion.29
  663.1 0.5 broadcast.700
  663.6 0.7 reduce.1
  664.5 0.9 reshape.2137
  665.4 3.5 all-to-all-start
  668.9 0.2 fusion.25
  669.5 0.7 reduce
  670.3 0.9 reshape.2135
  671.2 5.6 all-to-all-done
  676.8 3.5 all-to-all-start.1
  680.3 0.6 copy.118
  680.9 0.3 reshape.2138
  681.2 0.3 copy.99
  681.5 0.2 all_to_all.27
  681.7 6.4 all-to-all-done.1
  688.2 0.3 reshape.2136
  688.5 0.3 copy.101
  688.8 0.2 all_to_all.31
  689.1 1.3 copy.102
  (58 shorter events, 3.2 us)
Async XLA Ops:
  7.2 4.9 copy-start
  7.2 101.6 %all-reduce.3.cloned.1.call-start = ((), (), s32[]{:S(2)}) async-start(), calls=%async_computation.2 | async-start | bytes 2162688 | tf_op jit(solution)/shard_map/psum | solution.py:107
  10.3 1.7 copy-start.4
  10.4 1.7 copy-start.6
  108.7 1.6 copy-start.1
  113.9 1.0 copy-start.2
  637.5 1.0 copy-start.3
  647.3 9.4 %copy-start.5 = (bf16[1,2,256,1024]{3,2,1,0:T(8,128)(2,1)S(1)}, bf16[1,2,256,1024]{3,2,1,0:T(8,128)(2,1)}, u32[]{:S(2)}) copy-start(bf16[1,2,256,1024]{3,2,1,0:T(8,128)(2,1)} %param.7) | copy-start | bytes 3145732
  665.4 11.4 %all-to-all-start = ((bf16[16,2,2048]{2,1,0:T(2,128)(2,1)}), bf16[16,2,2048]{2,1,0:T(2,128)(2,1)S(1)}, u32[]{:S(2)}, u32[]{:S(2)}) async-start(bf16[16,2,2048]{2,1,0:T(2,128)(2,1)} %reshape.2137), calls=%async_computation | async-start | bytes 262144 | tf_op jit(solution)/shard_map/all_to_all | solution.py:129
  676.8 11.4 %all-to-all-start.1 = ((bf16[16,2,2048]{2,1,0:T(2,128)(2,1)}), bf16[16,2,2048]{2,1,0:T(2,128)(2,1)S(1)}, u32[]{:S(2)}, u32[]{:S(2)}) async-start(bf16[16,2,2048]{2,1,0:T(2,128)(2,1)} %reshape.2135), calls=%async_computation.1 | async-start | bytes 262144 | tf_op jit(solution)/shard_map/all_to_all | solution.py:129
Sparse Core Ops, SparseCore 0:
  12.1 96.5 all-reduce.2
where the time goes:
time: 704 us; the launch traced here: 697 us
  blocking collectives  486 us (69%)
  waiting for transfers between devices  107 us (15%)
  matrix products  43.8 us (6%)
  other arithmetic  29.7 us (4%)
  between operations  14.9 us (2%)
  local copies, waits for them, and re-layouts  9.1 us (1%)
  starting transfers between devices  7.06 us (1%)
    psum x7, blocking collectives, body(): summed = lax.psum(numerator, 'chan')  486 us
    psum x1, waiting for transfers between devices, body(): gram_all, summed = lax.psum((gram, numerator), 'chan')  94.6 us
    dot_general x8, matrix products, body(): jnp.einsum('kjs,jqs->kqs', inverse, summed, precision=HIGHEST)  28.4 us
  transfers between devices with their start and end apart: 3, of which 3 were waited for; matrix products, arithmetic and copies ran while one was open for 1% of the time, Pallas kernels for 0%

commit v1 on v0

v1 whole, which is shorter than its diff:
```python
import functools

import jax
import jax.numpy as jnp
import numpy as np
from jax import lax
from jax.experimental import pallas as pl
from jax.experimental.pallas import tpu as pltpu
from jax.sharding import PartitionSpec as P

ITERS = 8
ORDER = 4
PENALTY = 2.0
RIDGE = 1.0
VMEM = pltpu.VMEM
MIB = 1 << 20


def legendre(place):
    return [
        1.0,
        place,
        0.5 * (3.0 * place * place - 1.0),
        0.5 * (5.0 * place * place * place - 3.0 * place),
    ]


def basis_table(total):
    place = np.float32(2.0) * (np.arange(total, dtype=np.float32) + np.float32(0.5)) / np.float32(
        total
    ) - np.float32(1.0)
    return np.stack([np.broadcast_to(np.float32(v), place.shape) for v in legendre(place)], 1)


def whole(shape_count):
    return [pl.BlockSpec(memory_space=VMEM)] * shape_count


def pack_kernel(num_ref, weight_ref, flag_ref, out_ref):
    half = num_ref.shape[1] // 2
    mask = flag_ref[...].astype(jnp.float32)
    num = num_ref[...] * mask
    weight = weight_ref[...] * mask
    weight4 = jnp.concatenate([weight[0:1], weight[0:1], weight[1:2], weight[1:2]], 0)
    block = jnp.concatenate(
        [num[:, :half], num[:, half:], weight4[:, :half], weight4[:, half:]], 0
    )
    for peer in range(out_ref.shape[0]):
        out_ref[peer] = block


def pack(cal_num, cal_weight, flags, devices):
    stations = cal_num.shape[1]
    return pl.pallas_call(
        pack_kernel,
        out_shape=jax.ShapeDtypeStruct((devices, 16, stations // 2), jnp.float32),
        in_specs=whole(3),
        out_specs=pl.BlockSpec(memory_space=VMEM),
        compiler_params=pltpu.CompilerParams(vmem_limit_bytes=8 * MIB),
        name="pack",
    )(cal_num, cal_weight, flags)


def fit_polynomials():
    nodes = np.cos(np.pi * (np.arange(400) + 0.5) / 400) * 0.5
    square = nodes * nodes
    safe = np.sinc(nodes) * np.pi
    sine = np.polynomial.chebyshev.Chebyshev.fit(square, safe, 5, domain=[0, 0.25])
    cosine = np.polynomial.chebyshev.Chebyshev.fit(square, np.cos(np.pi * nodes), 5, domain=[0, 0.25])
    to_power = lambda c: c.convert(kind=np.polynomial.Polynomial).coef
    return [float(np.float32(v)) for v in to_power(sine)], [
        float(np.float32(v)) for v in to_power(cosine)
    ]


def horner(coefficients, x):
    value = coefficients[-1]
    for c in coefficients[-2::-1]:
        value = value * x + c
    return value


def phasor_kernel(rows, total, volts_ref, pos_ref, dir_ref, point_ref, cos_ref, sin_ref, rhs_ref, dirs):
    table = dir_ref.shape[1]
    beams = point_ref.shape[1]
    stations = pos_ref.shape[1]
    samples = volts_ref.shape[1]
    channel = lax.axis_index("chan").astype(jnp.float32)
    ratio = 1.0 + 0.3 * (channel + 0.5) / total

    d = dir_ref[...]
    high = d.astype(jnp.bfloat16)
    rest = d - high.astype(jnp.float32)
    middle = rest.astype(jnp.bfloat16)
    low = (rest - middle.astype(jnp.float32)).astype(jnp.bfloat16)
    zero = jnp.zeros_like(d)
    parts = jnp.concatenate(
        [high.astype(jnp.float32), middle.astype(jnp.float32), low.astype(jnp.float32), zero], 0
    ).astype(jnp.bfloat16)
    hot = (
        lax.broadcasted_iota(jnp.int32, (table, beams), 0) == point_ref[...]
    ).astype(jnp.float32).astype(jnp.bfloat16)
    found = jnp.dot(parts, hot, preferred_element_type=jnp.float32)
    exact = found[0:2] + found[2:4] + found[4:6]
    dirs[...] = jnp.transpose(jnp.concatenate([exact, exact, exact, exact], 0))

    half = samples // 2
    row = lax.broadcasted_iota(jnp.int32, (samples, samples), 0)
    column = lax.broadcasted_iota(jnp.int32, (samples, samples), 1)
    source = jnp.where(column < half, 2 * column, 2 * (column - half) + 1)
    spread = (row == source).astype(jnp.float32).astype(jnp.bfloat16)
    for polar in range(2):
        turned = lax.dot_general(
            volts_ref[polar], spread, (((0,), (0,)), ((), ())), preferred_element_type=jnp.float32
        )
        real, imag = turned[:stations], turned[stations:]
        rhs_ref[polar, :stations, :samples] = real.astype(jnp.bfloat16)
        rhs_ref[polar, stations:, :samples] = (-imag).astype(jnp.bfloat16)
        rhs_ref[polar, :stations, samples:] = imag.astype(jnp.bfloat16)
        rhs_ref[polar, stations:, samples:] = real.astype(jnp.bfloat16)

    sine_c, cosine_c = fit_polynomials()
    east = pos_ref[0:1, :] * ratio
    north = pos_ref[1:2, :] * ratio

    @pl.loop(0, beams // rows)
    def _(step):
        at = pl.ds(pl.multiple_of(step * rows, rows), rows)
        l = dirs[at, 0:1]
        m = dirs[at, 1:2]
        turns = l * east + m * north
        x = turns - jnp.round(turns)
        square = x * x
        s = x * horner(sine_c, square)
        c = horner(cosine_c, square)
        cos_ref[at, :] = 1.0 - 2.0 * (s * s)
        sin_ref[at, :] = 2.0 * (s * c)


def phasors(volts, positions, directions, pointing, total):
    beams = pointing.shape[1]
    stations = positions.shape[1]
    samples = volts.shape[1]
    return pl.pallas_call(
        functools.partial(phasor_kernel, 16, total),
        out_shape=(
            jax.ShapeDtypeStruct((beams, stations), jnp.float32),
            jax.ShapeDtypeStruct((beams, stations), jnp.float32),
            jax.ShapeDtypeStruct((2, 2 * stations, 2 * samples), jnp.bfloat16),
        ),
        in_specs=whole(4),
        out_specs=tuple(whole(3)),
        scratch_shapes=[pltpu.VMEM((beams, 8), jnp.float32)],
        compiler_params=pltpu.CompilerParams(vmem_limit_bytes=32 * MIB),
        cost_estimate=pl.CostEstimate(
            flops=60 * beams * stations, bytes_accessed=8 * MIB, transcendentals=0
        ),
        name="phasors",
    )(volts, positions, directions, pointing)


def invert_small(left):
    order = len(left)
    unit = jnp.ones_like(left[0][0])
    nothing = jnp.zeros_like(unit)
    right = [[unit if r == c else nothing for c in range(order)] for r in range(order)]
    for pivot in range(order):
        factor = 1.0 / left[pivot][pivot]
        left[pivot] = [entry * factor for entry in left[pivot]]
        right[pivot] = [entry * factor for entry in right[pivot]]
        for r in range(order):
            if r != pivot:
                scale = left[r][pivot]
                left[r] = [a - scale * b for a, b in zip(left[r], left[pivot])]
                right[r] = [a - scale * b for a, b in zip(right[r], right[pivot])]
    return right


def combine(weights, values):
    total = None
    for w, v in zip(weights, values):
        term = v if isinstance(w, float) and w == 1.0 else w * v
        total = term if total is None else total + term
    return total


def fit_kernel(cal_ref, out_ref, target, gain, mask_ref, dual, local):
    total = cal_ref.shape[0]
    half = cal_ref.shape[2]
    table = basis_table(total)
    rows = [[float(v) for v in line] for line in table]

    gram = [[None] * ORDER for _ in range(ORDER)]
    for c in range(total):
        weight = cal_ref[c, 8:16, :]
        mask = jnp.where(weight > 0.0, 1.0, 0.0)
        inverse = mask / (weight + PENALTY)
        target[c] = cal_ref[c, 0:8, :] * inverse
        gain[c] = PENALTY * inverse
        mask_ref[c] = mask
        dual[c] = jnp.zeros_like(mask)
        local[c] = jnp.zeros_like(mask)
        for k in range(ORDER):
            for j in range(k, ORDER):
                term = mask * (rows[c][k] * rows[c][j])
                gram[k][j] = term if gram[k][j] is None else gram[k][j] + term
    for k in range(ORDER):
        gram[k][k] = gram[k][k] + RIDGE
        for j in range(k):
            gram[k][j] = gram[j][k]
    inverse = invert_small(gram)

    def sweep(_, coefficients):
        sums = [None] * ORDER
        for c in range(total):
            fitted = combine(rows[c], coefficients)
            mask = mask_ref[c]
            d = dual[c] + (local[c] - mask * fitted)
            new = target[c] + gain[c] * (fitted - d)
            dual[c] = d
            local[c] = new
            u = new + d
            for k in range(ORDER):
                term = u if rows[c][k] == 1.0 else rows[c][k] * u
                sums[k] = term if sums[k] is None else sums[k] + term
        return tuple(combine(inverse[k], sums) for k in range(ORDER))

    zero = jnp.zeros((8, half), jnp.float32)
    coefficients = lax.fori_loop(0, ITERS, sweep, (zero,) * ORDER)
    channel = lax.axis_index("chan").astype(jnp.float32)
    place = 2.0 * (channel + 0.5) / total - 1.0
    fitted = combine(legendre(place), coefficients)
    out_ref[:, :half] = fitted[0:4]
    out_ref[:, half:] = fitted[4:8]


def fit(cal):
    total, _, half = cal.shape
    block = pltpu.VMEM((total, 8, half), jnp.float32)
    return pl.pallas_call(
        fit_kernel,
        out_shape=jax.ShapeDtypeStruct((4, 2 * half), jnp.float32),
        in_specs=whole(1),
        out_specs=pl.BlockSpec(memory_space=VMEM),
        scratch_shapes=[block] * 5,
        compiler_params=pltpu.CompilerParams(vmem_limit_bytes=16 * MIB),
        name="fit",
    )(cal)


def beam_kernel(fitted_ref, flag_ref, cos_ref, sin_ref, rhs_ref, out_ref):
    stations = cos_ref.shape[1]
    samples = rhs_ref.shape[2] // 2
    half = samples // 2
    scale = flag_ref[...].astype(jnp.float32) * stations ** (-0.5)
    gains = fitted_ref[...] * scale
    cosine = cos_ref[...]
    sine = sin_ref[...]
    power = None
    for polar in range(2):
        re = gains[2 * polar : 2 * polar + 1]
        im = gains[2 * polar + 1 : 2 * polar + 2]
        w_re = (re * cosine - im * sine).astype(jnp.bfloat16)
        w_im = (-(re * sine + im * cosine)).astype(jnp.bfloat16)
        lhs = jnp.concatenate([w_re, w_im], 1)
        y = jnp.dot(lhs, rhs_ref[polar], preferred_element_type=jnp.float32)
        y = y * y
        y = y[:, :samples] + y[:, samples:]
        power = y if power is None else power + y
    out_ref[...] = ((power[:, :half] + power[:, half:]) * 0.5).astype(jnp.bfloat16)


def beams_detect(fitted, flags, cosine, sine, rhs, rows):
    beams, stations = cosine.shape
    samples = rhs.shape[2] // 2
    fixed = lambda *shape: pl.BlockSpec(shape, lambda i: (0,) * len(shape))
    return pl.pallas_call(
        beam_kernel,
        grid=(beams // rows,),
        out_shape=jax.ShapeDtypeStruct((beams, samples // 2), jnp.bfloat16),
        in_specs=[
            fixed(4, stations),
            fixed(1, stations),
            pl.BlockSpec((rows, stations), lambda i: (i, 0)),
            pl.BlockSpec((rows, stations), lambda i: (i, 0)),
            fixed(2, 2 * stations, 2 * samples),
        ],
        out_specs=pl.BlockSpec((rows, samples // 2), lambda i: (i, 0)),
        compiler_params=pltpu.CompilerParams(vmem_limit_bytes=32 * MIB),
        name="beams",
    )(fitted, flags, cosine, sine, rhs)


def body(voltages, cal_num, cal_weight, flags, positions, directions, pointing):
    devices = lax.axis_size("chan")
    assert voltages.shape[0] == 1
    total = devices
    packed = pack(cal_num[0], cal_weight[0], flags, devices)
    cal = lax.all_to_all(packed, "chan", 0, 0, tiled=True)
    cosine, sine, rhs = phasors(voltages[0], positions, directions, pointing[None, :], total)
    fitted = fit(cal)
    power = beams_detect(fitted, flags, cosine, sine, rhs, 256)
    moved = lax.all_to_all(power, "chan", 0, 0, tiled=True)
    beams = power.shape[0] // devices
    beam_power = jnp.transpose(moved.reshape(devices, beams, power.shape[1]), (1, 0, 2))
    return beam_power, fitted[None]


def solution(mesh):
    return jax.shard_map(
        body,
        mesh=mesh,
        in_specs=(
            P(("group", "chan"), None, None, None),
            P(("group", "chan"), None, None),
            P(("group", "chan"), None, None),
            P(("group", "chan"), None),
            P(),
            P(),
            P("group"),
        ),
        out_specs=(P(("group", "chan"), None, None), P(("group", "chan"), None, None)),
        check_vma=False,
    )
```

time: 704 us -> 50.6 us (0.07)
  blocking collectives: 486 us -> 15.8 us
  waiting for transfers between devices: 107 us -> 0.01 us
  matrix products: 43.8 us -> 0 us
  other arithmetic: 29.7 us -> 0 us
  between operations: 14.9 us -> 0.7 us
  Pallas kernels: 0 us -> 13.2 us
    psum x7 -> x0, blocking collectives: 486 us -> none  [body(): summed = lax.psum(numerator, 'chan')]
    psum x1 -> x0, waiting for transfers between devices: 94.6 us -> none  [body(): gram_all, summed = lax.psum((gram, numerator), 'chan')]
    dot_general x21 -> x0, matrix products: 43.8 us -> none  [the longest x8 28.4 us: body(): jnp.einsum('kjs,jqs->kqs', inverse, summed, precision=HIGHEST)]
    all_to_all x0 -> x1, blocking collectives: none -> 15.8 us  [body(): moved = lax.all_to_all(power, 'chan', 0, 0, tiled=True)]
    pallas_call x0 -> x4, Pallas kernels: none -> 13.2 us  [the longest x1 7.69 us: phasors(): pl.pallas_call(functools.partial(phasor_kernel, 16, total), out_shape=(ja...]
    all_to_all x2 -> x1, waiting for transfers between devices: 12 us -> 0.01 us  [body(): cal = lax.all_to_all(packed, 'chan', 0, 0, tiled=True)]
    convert_element_type x7 -> x0, other arithmetic: 11.4 us -> none  [the longest x1 9.35 us: beam_matrices(): w_im = (-(gain_re * sine + gain_im * cosine)).astype(jnp.bfloat16)]
    neg x1 -> x0, other arithmetic: 8.79 us -> none  [beam_matrices(): upper = jnp.concatenate([w_re, -w_im], axis=1)]
  transfers between devices with their start and end apart: 3 -> 1, of which waited for: 3 -> 0; matrix products, arithmetic and copies ran while one was open for 1% -> 0% of each run, Pallas kernels for 0% -> 15%
where the time goes in v1:
time: 50.6 us; the launch traced here: 50 us
  blocking collectives  15.8 us (31%)
  Pallas kernels  13.2 us (26%)
  local copies, waits for them, and re-layouts  12.8 us (25%)
  starting transfers between devices  7.41 us (15%)
  between operations  0.7 us (1%)
    all_to_all x1, blocking collectives, body(): moved = lax.all_to_all(power, 'chan', 0, 0, tiled=True)  15.8 us
    unnamed x27, local copies, waits for them, and re-layouts  12.8 us
    pallas_call x1, Pallas kernels, phasors(): pl.pallas_call(functools.partial(phasor_kernel, 16, total), out_shape=(ja...  7.69 us
    all_to_all x1, starting transfers between devices, body(): cal = lax.all_to_all(packed, 'chan', 0, 0, tiled=True)  7.41 us
    pallas_call x1, Pallas kernels, beams_detect(): pl.pallas_call(beam_kernel, grid=(beams // rows,), out_shape=jax.ShapeDty...  3.23 us
    pallas_call x1, Pallas kernels, fit(): pl.pallas_call(fit_kernel, out_shape=jax.ShapeDtypeStruct((4, 2 * half),...  1.55 us
  transfers between devices with their start and end apart: 1, of which 0 were waited for; matrix products, arithmetic and copies ran while one was open for 0% of the time, Pallas kernels for 15%

profile of v1, /device:TPU:0, one launch (start us, length us, event | category | flops | bytes accessed | tf_op | source)
XLA Modules:
  0.0 50.0 jit_solution(797566913229283814)
XLA Ops:
  0.6 0.0 copy-start.8
  0.6 0.0 copy-start.7
  0.7 0.7 %copy-done.7 = s32[1,512]{1,0:T(1,128)S(1)} copy-done((s32[1,512]{1,0:T(1,128)S(1)}, s32[1,512]{1,0:T(1,128)}, u32[]{:S(2)}) %copy-start.7) | copy-done | bytes 2072
  1.4 0.0 copy-start.9
  1.4 0.7 %copy-done.9 = f32[1,4,512]{2,1,0:T(4,128)S(1)} copy-done((f32[1,4,512]{2,1,0:T(4,128)S(1)}, f32[1,4,512]{2,1,0:T(4,128)}, u32[]{:S(2)}) %copy-start.9) | copy-done | bytes 8216
  2.1 0.0 copy-start.10
  2.1 0.7 %copy-done.10 = f32[1,2,512]{2,1,0:T(2,128)S(1)} copy-done((f32[1,2,512]{2,1,0:T(2,128)S(1)}, f32[1,2,512]{2,1,0:T(2,128)}, u32[]{:S(2)}) %copy-start.10) | copy-done | bytes 4120
  2.8 0.7 %pack.1 = f32[16,16,256]{2,1,0:T(8,128)} custom-call(f32[4,512]{1,0:T(4,128)S(1)} %bitcast.10, f32[2,512]{1,0:T(2,128)S(1)} %bitcast.11, s32[1,512]{1,0:T(1,128)S(1)} %copy-done.7), custom_call_target="tpu_custom_call" | custom-call | tf_op jit(solution)/shard_map/pack/pallas_call | solution.py:54
  3.5 7.4 %all-to-all-start = ((f32[16,16,256]{2,1,0:T(8,128)}), f32[16,16,256]{2,1,0:T(8,128)S(1)}, u32[]{:S(2)}, u32[]{:S(2)}) async-start(f32[16,16,256]{2,1,0:T(8,128)} %pack.1), calls=%async_computation | async-start | bytes 524288 | tf_op jit(solution)/shard_map/all_to_all | solution.py:299
  10.9 0.0 copy-start.4
  10.9 1.2 %copy-done.4 = bf16[1,2,256,1024]{3,2,1,0:T(8,128)(2,1)S(1)} copy-done((bf16[1,2,256,1024]{3,2,1,0:T(8,128)(2,1)S(1)}, bf16[1,2,256,1024]{3,2,1,0:T(8,128)(2,1)}, u32[]{:S(2)}) %copy-start.4) | copy-done | bytes 1048600
  12.2 0.0 copy-start.6
  12.2 0.7 %copy-done.6 = f32[2,1024]{1,0:T(2,128)S(1)} copy-done((f32[2,1024]{1,0:T(2,128)S(1)}, f32[2,1024]{1,0:T(2,128)}, u32[]{:S(2)}) %copy-start.6) | copy-done | bytes 8216
  12.9 0.0 copy-start.11
  12.9 0.7 %copy-done.11 = f32[2,512]{1,0:T(2,128)S(1)} copy-done((f32[2,512]{1,0:T(2,128)S(1)}, f32[2,512]{1,0:T(2,128)}, u32[]{:S(2)}) %copy-start.11) | copy-done | bytes 4120
  13.5 0.0 copy-start.12
  13.5 0.7 %copy-done.12 = s32[1024]{0:T(1024)S(1)} copy-done((s32[1024]{0:T(1024)S(1)}, s32[1024]{0:T(1024)}, u32[]{:S(2)}) %copy-start.12) | copy-done | bytes 4120
  14.2 7.7 %phasors.1 = (f32[1024,512]{1,0:T(8,128)S(1)}, f32[1024,512]{1,0:T(8,128)S(1)}, bf16[2,1024,512]{2,1,0:T(8,128)(2,1)S(1)}) custom-call(bf16[2,256,1024]{2,1,0:T(8,128)(2,1)S(1)} %bitcast.8, f32[2,512]{1,0:T(2,128)S(1)} %copy-done.11, f32[2,1024]{1,0:T(2,128)S(1)} %copy-done.6, s32[1,1024]{1,0:T(1,128)S(1)} %bitcast.12), custom_call_target="tpu_custom_call" | custom-call | flops 31457280 | bytes 8388608 | tf_op jit(solution)/shard_map/phasors/pallas_call | solution.py:144
  21.9 0.0 copy-start
  21.9 1.3 %copy-done = f32[1024,512]{1,0:T(8,128)} copy-done((f32[1024,512]{1,0:T(8,128)}, f32[1024,512]{1,0:T(8,128)S(1)}, u32[]{:S(2)}) %copy-start) | copy-done | bytes 2097176
  23.3 0.0 copy-start.2
  23.3 1.3 %copy-done.2 = bf16[2,1024,512]{2,1,0:T(8,128)(2,1)} copy-done((bf16[2,1024,512]{2,1,0:T(8,128)(2,1)}, bf16[2,1024,512]{2,1,0:T(8,128)(2,1)S(1)}, u32[]{:S(2)}) %copy-start.2) | copy-done | bytes 2097176
  24.6 0.0 all-to-all-done.cal_ref
  24.6 1.5 %fit.1.fitted_ref = f32[4,512]{1,0:T(4,128)} custom-call(f32[16,16,256]{2,1,0:T(8,128)S(1)} %all-to-all-done.cal_ref), custom_call_target="tpu_custom_call" | custom-call | tf_op jit(solution)/shard_map/fit/pallas_call | solution.py:240
  26.1 0.0 copy-done.8
  26.1 0.0 copy-start.1
  26.1 1.6 %copy-done.1 = f32[1024,512]{1,0:T(8,128)S(1)} copy-done((f32[1024,512]{1,0:T(8,128)S(1)}, f32[1024,512]{1,0:T(8,128)}, u32[]{:S(2)}) %copy-start.1) | copy-done | bytes 2097176
  27.7 0.0 copy-start.3
  27.7 1.6 %copy-done.3 = bf16[2,1024,512]{2,1,0:T(8,128)(2,1)S(1)} copy-done((bf16[2,1024,512]{2,1,0:T(8,128)(2,1)S(1)}, bf16[2,1024,512]{2,1,0:T(8,128)(2,1)}, u32[]{:S(2)}) %copy-start.3) | copy-done | bytes 2097176
  29.3 0.0 copy-start.5
  29.3 0.7 %copy-done.5 = f32[4,512]{1,0:T(4,128)S(1)} copy-done((f32[4,512]{1,0:T(4,128)S(1)}, f32[4,512]{1,0:T(4,128)}, u32[]{:S(2)}) %copy-start.5) | copy-done | bytes 8216
  30.0 3.2 %beams.1 = bf16[1024,128]{1,0:T(8,128)(2,1)S(1)} custom-call(f32[4,512]{1,0:T(4,128)S(1)} %copy-done.5, s32[1,512]{1,0:T(1,128)S(1)} %copy-done.8, f32[1024,512]{1,0:T(8,128)S(1)} %get-tuple-element.5.cos_ref, f32[1024,512]{1,0:T(8,128)S(1)} %copy-done.1, bf16[2,1024,512]{2,1,0:T(8,128)(2,1)S(1)} %copy-done.3), custom_call_target="tpu_custom_call" | custom-call | tf_op jit(solution)/shard_map/beams/pallas_call | solution.py:277
  33.2 15.8 %all_to_all.14 = bf16[16,64,128]{2,1,0:T(8,128)(2,1)S(1)} all-to-all(bf16[16,64,128]{2,1,0:T(8,128)(2,1)S(1)} %bitcast.7), channel_id=1, replica_groups=mesh['group'=2,'chan'=16] {'chan'}, dimensions={0} | all-to-all | bytes 524288 | tf_op jit(solution)/shard_map/all_to_all | solution.py:303
  49.1 0.9 %copy.10 = bf16[64,16,128]{2,1,0:T(8,128)(2,1)} copy(bf16[64,16,128]{2,0,1:T(8,128)(2,1)S(1)} %bitcast.13) | data formatting | bytes 524288
Async XLA Ops:
  0.6 25.5 %copy-start.8 = (s32[1,512]{1,0:T(1,128)S(1)}, s32[1,512]{1,0:T(1,128)}, u32[]{:S(2)}) copy-start(s32[1,512]{1,0:T(1,128)} %flag_ref.3) | copy-start | bytes 6148
  0.6 0.7 %copy-start.7 = (s32[1,512]{1,0:T(1,128)S(1)}, s32[1,512]{1,0:T(1,128)}, u32[]{:S(2)}) copy-start(s32[1,512]{1,0:T(1,128)} %flag_ref.3) | copy-start | bytes 6148
  1.4 0.7 %copy-start.9 = (f32[1,4,512]{2,1,0:T(4,128)S(1)}, f32[1,4,512]{2,1,0:T(4,128)}, u32[]{:S(2)}) copy-start(f32[1,4,512]{2,1,0:T(4,128)} %param.8) | copy-start | bytes 24580
  2.1 0.7 %copy-start.10 = (f32[1,2,512]{2,1,0:T(2,128)S(1)}, f32[1,2,512]{2,1,0:T(2,128)}, u32[]{:S(2)}) copy-start(f32[1,2,512]{2,1,0:T(2,128)} %param.9) | copy-start | bytes 12292
  3.5 21.1 %all-to-all-start = ((f32[16,16,256]{2,1,0:T(8,128)}), f32[16,16,256]{2,1,0:T(8,128)S(1)}, u32[]{:S(2)}, u32[]{:S(2)}) async-start(f32[16,16,256]{2,1,0:T(8,128)} %pack.1), calls=%async_computation | async-start | bytes 524288 | tf_op jit(solution)/shard_map/all_to_all | solution.py:299
  10.9 1.2 %copy-start.4 = (bf16[1,2,256,1024]{3,2,1,0:T(8,128)(2,1)S(1)}, bf16[1,2,256,1024]{3,2,1,0:T(8,128)(2,1)}, u32[]{:S(2)}) copy-start(bf16[1,2,256,1024]{3,2,1,0:T(8,128)(2,1)} %param.7) | copy-start | bytes 3145732
  12.2 0.7 %copy-start.6 = (f32[2,1024]{1,0:T(2,128)S(1)}, f32[2,1024]{1,0:T(2,128)}, u32[]{:S(2)}) copy-start(f32[2,1024]{1,0:T(2,128)} %dir_ref.1) | copy-start | bytes 24580
  12.9 0.7 %copy-start.11 = (f32[2,512]{1,0:T(2,128)S(1)}, f32[2,512]{1,0:T(2,128)}, u32[]{:S(2)}) copy-start(f32[2,512]{1,0:T(2,128)} %pos_ref.1) | copy-start | bytes 12292
  13.5 0.7 %copy-start.12 = (s32[1024]{0:T(1024)S(1)}, s32[1024]{0:T(1024)}, u32[]{:S(2)}) copy-start(s32[1024]{0:T(1024)} %param.13) | copy-start | bytes 12292
  21.9 1.3 %copy-start = (f32[1024,512]{1,0:T(8,128)}, f32[1024,512]{1,0:T(8,128)S(1)}, u32[]{:S(2)}) copy-start(f32[1024,512]{1,0:T(8,128)S(1)} %get-tuple-element.6.sin_ref) | copy-start | bytes 6291460
  23.3 1.3 %copy-start.2 = (bf16[2,1024,512]{2,1,0:T(8,128)(2,1)}, bf16[2,1024,512]{2,1,0:T(8,128)(2,1)S(1)}, u32[]{:S(2)}) copy-start(bf16[2,1024,512]{2,1,0:T(8,128)(2,1)S(1)} %get-tuple-element.7.rhs_ref) | copy-start | bytes 6291460
  26.1 1.6 %copy-start.1 = (f32[1024,512]{1,0:T(8,128)S(1)}, f32[1024,512]{1,0:T(8,128)}, u32[]{:S(2)}) copy-start(f32[1024,512]{1,0:T(8,128)} %copy-done) | copy-start | bytes 6291460
  27.7 1.6 %copy-start.3 = (bf16[2,1024,512]{2,1,0:T(8,128)(2,1)S(1)}, bf16[2,1024,512]{2,1,0:T(8,128)(2,1)}, u32[]{:S(2)}) copy-start(bf16[2,1024,512]{2,1,0:T(8,128)(2,1)} %copy-done.2) | copy-start | bytes 6291460
  29.3 0.7 %copy-start.5 = (f32[4,512]{1,0:T(4,128)S(1)}, f32[4,512]{1,0:T(4,128)}, u32[]{:S(2)}) copy-start(f32[4,512]{1,0:T(4,128)} %fit.1.fitted_ref) | copy-start | bytes 24580

commit v2 on v1

v2 whole, which is shorter than its diff:
```python
import functools

import jax
import jax.numpy as jnp
import numpy as np
from jax import lax
from jax.experimental import pallas as pl
from jax.experimental.pallas import tpu as pltpu
from jax.sharding import PartitionSpec as P

ITERS = 8
ORDER = 4
PENALTY = 2.0
RIDGE = 1.0
MIB = 1 << 20
GRANT = 67_000_000


def legendre(place):
    return [
        1.0,
        place,
        0.5 * (3.0 * place * place - 1.0),
        0.5 * (5.0 * place * place * place - 3.0 * place),
    ]


def basis_table(total):
    place = np.float32(2.0) * (np.arange(total, dtype=np.float32) + np.float32(0.5)) / np.float32(
        total
    ) - np.float32(1.0)
    return np.stack([np.broadcast_to(np.float32(v), place.shape) for v in legendre(place)], 1)


HBM_SPEC = pl.BlockSpec(memory_space=pltpu.HBM)
VMEM_SPEC = pl.BlockSpec(memory_space=pltpu.VMEM)


def start(source, target, semaphore):
    copy = pltpu.make_async_copy(source, target, semaphore)
    copy.start()
    return copy


def pack_kernel(num_hbm, weight_hbm, flag_hbm, out_ref, num_ref, weight_ref, flag_ref, sems):
    copies = [
        start(num_hbm, num_ref, sems.at[0]),
        start(weight_hbm, weight_ref, sems.at[1]),
        start(flag_hbm, flag_ref, sems.at[2]),
    ]
    for copy in copies:
        copy.wait()
    half = num_ref.shape[1] // 2
    mask = flag_ref[...].astype(jnp.float32)
    num = num_ref[...] * mask
    weight = weight_ref[...] * mask
    weight4 = jnp.concatenate([weight[0:1], weight[0:1], weight[1:2], weight[1:2]], 0)
    block = jnp.concatenate(
        [num[:, :half], num[:, half:], weight4[:, :half], weight4[:, half:]], 0
    )
    for peer in range(out_ref.shape[0]):
        out_ref[peer] = block


def pack(cal_num, cal_weight, flags, devices):
    stations = cal_num.shape[1]
    return pl.pallas_call(
        pack_kernel,
        out_shape=jax.ShapeDtypeStruct((devices, 16, stations // 2), jnp.float32),
        in_specs=[HBM_SPEC] * 3,
        out_specs=VMEM_SPEC,
        scratch_shapes=[
            pltpu.VMEM(cal_num.shape, jnp.float32),
            pltpu.VMEM(cal_weight.shape, jnp.float32),
            pltpu.VMEM(flags.shape, jnp.int32),
            pltpu.SemaphoreType.DMA((3,)),
        ],
        compiler_params=pltpu.CompilerParams(vmem_limit_bytes=GRANT),
        name="pack",
    )(cal_num, cal_weight, flags)


def fit_polynomials():
    nodes = np.cos(np.pi * (np.arange(400) + 0.5) / 400) * 0.5
    square = nodes * nodes
    safe = np.sinc(nodes) * np.pi
    chebyshev = np.polynomial.chebyshev.Chebyshev
    sine = chebyshev.fit(square, safe, 4, domain=[0, 0.25])
    cosine = chebyshev.fit(square, np.cos(np.pi * nodes), 5, domain=[0, 0.25])
    to_power = lambda c: c.convert(kind=np.polynomial.Polynomial).coef * np.sqrt(2.0)
    return [float(np.float32(v)) for v in to_power(sine)], [
        float(np.float32(v)) for v in to_power(cosine)
    ]


def horner(coefficients, x):
    value = coefficients[-1]
    for c in coefficients[-2::-1]:
        value = value * x + c
    return value


def phasor_kernel(
    rows, blocks, total, volts_hbm, pos_hbm, dir_hbm, point_hbm, phase_hbm, rhs_hbm,
    volts_ref, pos_ref, dir_ref, point_ref, phase_ref, rhs_ref, dirs, sems, out_sems,
):
    incoming = [
        start(point_hbm, point_ref, sems.at[0]),
        start(dir_hbm, dir_ref, sems.at[1]),
        start(pos_hbm, pos_ref, sems.at[2]),
        start(volts_hbm, volts_ref, sems.at[3]),
    ]
    table = dir_ref.shape[1]
    beams = point_ref.shape[1]
    stations = pos_ref.shape[1]
    samples = volts_ref.shape[1]
    channel = lax.axis_index("chan").astype(jnp.float32)
    ratio = 1.0 + 0.3 * (channel + 0.5) / total
    for copy in incoming[:3]:
        copy.wait()

    d = dir_ref[...]
    high = d.astype(jnp.bfloat16).astype(jnp.float32)
    middle = (d - high).astype(jnp.bfloat16).astype(jnp.float32)
    low = d - high - middle
    parts = jnp.concatenate([high, middle, low, jnp.zeros_like(d)], 0).astype(jnp.bfloat16)
    hot = (
        (lax.broadcasted_iota(jnp.int32, (table, beams), 0) == point_ref[...])
        .astype(jnp.float32)
        .astype(jnp.bfloat16)
    )
    found = jnp.dot(parts, hot, preferred_element_type=jnp.float32)
    exact = found[0:2] + found[2:4] + found[4:6]
    dirs[...] = jnp.transpose(jnp.concatenate([exact] * 4, 0))

    sine_c, cosine_c = fit_polynomials()
    east = pos_ref[0:1, :] * ratio
    north = pos_ref[1:2, :] * ratio
    magic = 12582912.0
    per_block = beams // blocks
    outgoing = []
    for block in range(blocks):

        @pl.loop(0, per_block // rows, unroll=2)
        def _(step):
            at = pl.ds(pl.multiple_of(block * per_block + step * rows, rows), rows)
            turns = dirs[at, 0:1] * east + dirs[at, 1:2] * north
            x = turns - ((turns + magic) - magic)
            square = x * x
            s = x * horner(sine_c, square)
            c = horner(cosine_c, square)
            phase_ref[0, at, :] = 1.0 - s * s
            phase_ref[1, at, :] = s * c

        part = pl.ds(block * per_block, per_block)
        outgoing.append(start(phase_ref.at[:, part], phase_hbm.at[:, part], out_sems.at[block]))

    incoming[3].wait()
    half = samples // 2
    row = lax.broadcasted_iota(jnp.int32, (samples, samples), 0)
    column = lax.broadcasted_iota(jnp.int32, (samples, samples), 1)
    source = jnp.where(column < half, 2 * column, 2 * (column - half) + 1)
    spread = (row == source).astype(jnp.float32).astype(jnp.bfloat16)
    for polar in range(2):
        turned = lax.dot_general(
            volts_ref[polar], spread, (((0,), (0,)), ((), ())), preferred_element_type=jnp.float32
        )
        real, imag = turned[:stations], turned[stations:]
        rhs_ref[polar, :stations, :samples] = real.astype(jnp.bfloat16)
        rhs_ref[polar, stations:, :samples] = (-imag).astype(jnp.bfloat16)
        rhs_ref[polar, :stations, samples:] = imag.astype(jnp.bfloat16)
        rhs_ref[polar, stations:, samples:] = real.astype(jnp.bfloat16)
        outgoing.append(start(rhs_ref.at[polar], rhs_hbm.at[polar], out_sems.at[blocks + polar]))
    for copy in outgoing:
        copy.wait()


def phasors(volts, positions, directions, pointing, total):
    beams = pointing.shape[1]
    stations = positions.shape[1]
    samples = volts.shape[1]
    blocks = 4
    phase = (2, beams, stations)
    rhs = (2, 2 * stations, 2 * samples)
    return pl.pallas_call(
        functools.partial(phasor_kernel, 16, blocks, total),
        out_shape=(
            jax.ShapeDtypeStruct(phase, jnp.float32),
            jax.ShapeDtypeStruct(rhs, jnp.bfloat16),
        ),
        in_specs=[HBM_SPEC] * 4,
        out_specs=(HBM_SPEC, HBM_SPEC),
        scratch_shapes=[
            pltpu.VMEM(volts.shape, volts.dtype),
            pltpu.VMEM(positions.shape, jnp.float32),
            pltpu.VMEM(directions.shape, jnp.float32),
            pltpu.VMEM(pointing.shape, jnp.int32),
            pltpu.VMEM(phase, jnp.float32),
            pltpu.VMEM(rhs, jnp.bfloat16),
            pltpu.VMEM((beams, 8), jnp.float32),
            pltpu.SemaphoreType.DMA((4,)),
            pltpu.SemaphoreType.DMA((blocks + 2,)),
        ],
        compiler_params=pltpu.CompilerParams(vmem_limit_bytes=GRANT),
        cost_estimate=pl.CostEstimate(
            flops=60 * beams * stations, bytes_accessed=8 * MIB, transcendentals=0
        ),
        name="phasors",
    )(volts, positions, directions, pointing)


def invert_small(left):
    order = len(left)
    unit = jnp.ones_like(left[0][0])
    nothing = jnp.zeros_like(unit)
    right = [[unit if r == c else nothing for c in range(order)] for r in range(order)]
    for pivot in range(order):
        factor = 1.0 / left[pivot][pivot]
        left[pivot] = [entry * factor for entry in left[pivot]]
        right[pivot] = [entry * factor for entry in right[pivot]]
        for r in range(order):
            if r != pivot:
                scale = left[r][pivot]
                left[r] = [a - scale * b for a, b in zip(left[r], left[pivot])]
                right[r] = [a - scale * b for a, b in zip(right[r], right[pivot])]
    return right


def combine(weights, values):
    total = None
    for w, v in zip(weights, values):
        term = v if isinstance(w, float) and w == 1.0 else w * v
        total = term if total is None else total + term
    return total


def solve(cal_ref, target, gain, mask_ref, dual, local):
    total = cal_ref.shape[0]
    half = cal_ref.shape[2]
    rows = [[float(v) for v in line] for line in basis_table(total)]

    gram = [[None] * ORDER for _ in range(ORDER)]
    for c in range(total):
        weight = cal_ref[c, 8:16, :]
        mask = jnp.where(weight > 0.0, 1.0, 0.0)
        inverse = mask / (weight + PENALTY)
        target[c] = cal_ref[c, 0:8, :] * inverse
        gain[c] = PENALTY * inverse
        mask_ref[c] = mask
        dual[c] = jnp.zeros_like(mask)
        local[c] = jnp.zeros_like(mask)
        for k in range(ORDER):
            for j in range(k, ORDER):
                term = mask * (rows[c][k] * rows[c][j])
                gram[k][j] = term if gram[k][j] is None else gram[k][j] + term
    for k in range(ORDER):
        gram[k][k] = gram[k][k] + RIDGE
        for j in range(k):
            gram[k][j] = gram[j][k]
    inverse = invert_small(gram)

    def sweep(_, coefficients):
        sums = [None] * ORDER
        for c in range(total):
            fitted = combine(rows[c], coefficients)
            d = dual[c] + (local[c] - mask_ref[c] * fitted)
            new = target[c] + gain[c] * (fitted - d)
            dual[c] = d
            local[c] = new
            u = new + d
            for k in range(ORDER):
                term = u if rows[c][k] == 1.0 else rows[c][k] * u
                sums[k] = term if sums[k] is None else sums[k] + term
        return tuple(combine(inverse[k], sums) for k in range(ORDER))

    zero = jnp.zeros((8, half), jnp.float32)
    coefficients = lax.fori_loop(0, ITERS, sweep, (zero,) * ORDER)
    channel = lax.axis_index("chan").astype(jnp.float32)
    place = 2.0 * (channel + 0.5) / total - 1.0
    return combine(legendre(place), coefficients)


def beam_kernel(
    blocks, cal_ref, phase_hbm, rhs_hbm, out_ref, fitted_ref,
    phase_ref, rhs_ref, target, gain, mask_ref, dual, local, sems,
):
    stations = phase_ref.shape[2]
    samples = rhs_ref.shape[2] // 2
    half = samples // 2
    per_block = phase_ref.shape[1] // blocks
    rhs_copy = start(rhs_hbm, rhs_ref, sems.at[0])
    phase_copies = []
    for block in range(blocks):
        part = pl.ds(block * per_block, per_block)
        phase_copies.append(start(phase_hbm.at[:, part], phase_ref.at[:, part], sems.at[1 + block]))

    fitted = solve(cal_ref, target, gain, mask_ref, dual, local)
    fitted_ref[:, : stations // 2] = fitted[0:4]
    fitted_ref[:, stations // 2 :] = fitted[4:8]
    dense = fitted * (mask_ref[lax.axis_index("chan")] * stations ** (-0.5))
    gains = jnp.concatenate([dense[0:4], dense[4:8]], 1)
    rhs_copy.wait()
    for block in range(blocks):
        part = pl.ds(block * per_block, per_block)
        phase_copies[block].wait()
        cosine = phase_ref[0, part]
        sine = phase_ref[1, part]
        power = None
        for polar in range(2):
            re = gains[2 * polar : 2 * polar + 1]
            im = gains[2 * polar + 1 : 2 * polar + 2]
            w_re = (re * cosine - im * sine).astype(jnp.bfloat16)
            w_im = (-(re * sine + im * cosine)).astype(jnp.bfloat16)
            lhs = jnp.concatenate([w_re, w_im], 1)
            y = jnp.dot(lhs, rhs_ref[polar], preferred_element_type=jnp.float32)
            y = y * y
            y = y[:, :samples] + y[:, samples:]
            power = y if power is None else power + y
        out_ref[part, :] = ((power[:, :half] + power[:, half:]) * 0.5).astype(jnp.bfloat16)


def fit_and_detect(cal, phase, rhs):
    total, _, half_stations = cal.shape
    _, beams, stations = phase.shape
    samples = rhs.shape[2] // 2
    blocks = 4
    state = pltpu.VMEM((total, 8, half_stations), jnp.float32)
    return pl.pallas_call(
        functools.partial(beam_kernel, blocks),
        out_shape=(
            jax.ShapeDtypeStruct((beams, samples // 2), jnp.bfloat16),
            jax.ShapeDtypeStruct((4, stations), jnp.float32),
        ),
        in_specs=[VMEM_SPEC, HBM_SPEC, HBM_SPEC],
        out_specs=(VMEM_SPEC, VMEM_SPEC),
        scratch_shapes=[
            pltpu.VMEM(phase.shape, jnp.float32),
            pltpu.VMEM(rhs.shape, jnp.bfloat16),
        ]
        + [state] * 5
        + [pltpu.SemaphoreType.DMA((1 + blocks,))],
        compiler_params=pltpu.CompilerParams(vmem_limit_bytes=GRANT - MIB),
        name="beams",
    )(cal, phase, rhs)


def body(voltages, cal_num, cal_weight, flags, positions, directions, pointing):
    devices = lax.axis_size("chan")
    assert voltages.shape[0] == 1
    total = devices
    packed = pack(cal_num[0], cal_weight[0], flags, devices)
    cal = lax.all_to_all(packed, "chan", 0, 0, tiled=True)
    phase, rhs = phasors(voltages[0], positions, directions, pointing[None, :], total)
    power, fitted = fit_and_detect(cal, phase, rhs)
    moved = lax.all_to_all(power, "chan", 0, 0, tiled=True)
    beams = power.shape[0] // devices
    beam_power = jnp.transpose(moved.reshape(devices, beams, power.shape[1]), (1, 0, 2))
    return beam_power, fitted[None]


def solution(mesh):
    return jax.shard_map(
        body,
        mesh=mesh,
        in_specs=(
            P(("group", "chan"), None, None, None),
            P(("group", "chan"), None, None),
            P(("group", "chan"), None, None),
            P(("group", "chan"), None),
            P(),
            P(),
            P("group"),
        ),
        out_specs=(P(("group", "chan"), None, None), P(("group", "chan"), None, None)),
        check_vma=False,
    )
```

time: 50.6 us -> 41.1 us (0.81)
  local copies, waits for them, and re-layouts: 12.8 us -> 0.88 us
  waiting for transfers between devices: 0.01 us -> 2.57 us
  Pallas kernels: 13.2 us -> 15.5 us
  blocking collectives: 15.8 us -> 13.5 us
    unnamed x27 -> x1, local copies, waits for them, and re-layouts: 12.8 us -> 0.88 us
    all_to_all x1, waiting for transfers between devices: 0.01 us -> 2.57 us  [body(): cal = lax.all_to_all(packed, 'chan', 0, 0, tiled=True)]
    all_to_all x1, blocking collectives: 15.8 us -> 13.5 us  [body(): moved = lax.all_to_all(power, 'chan', 0, 0, tiled=True)]
    pallas_call x3 -> x2, Pallas kernels: 12.5 us -> 14 us  [the longest x1 7.49 us: phasors(): pl.pallas_call(functools.partial(phasor_kernel, 16, blocks, total), out_s...]
    pallas_call x1, Pallas kernels: 0.73 us -> 1.47 us  [pack(): pl.pallas_call(pack_kernel, out_shape=jax.ShapeDtypeStruct((devices, 16,...]
  transfers between devices with their start and end apart: 1 -> 1, of which waited for: 0 -> 1; matrix products, arithmetic and copies ran while one was open for 0% -> 0% of each run, Pallas kernels for 15% -> 18%
where the time goes in v2:
time: 41.1 us; the launch traced here: 40.6 us
  Pallas kernels  15.5 us (38%)
  blocking collectives  13.5 us (33%)
  starting transfers between devices  7.48 us (18%)
  waiting for transfers between devices  2.57 us (6%)
  local copies, waits for them, and re-layouts  0.88 us (2%)
  between operations  0.66 us (2%)
    all_to_all x1, blocking collectives, body(): moved = lax.all_to_all(power, 'chan', 0, 0, tiled=True)  13.5 us
    pallas_call x1, Pallas kernels, phasors(): pl.pallas_call(functools.partial(phasor_kernel, 16, blocks, total), out_s...  7.49 us
    all_to_all x1, starting transfers between devices, body(): cal = lax.all_to_all(packed, 'chan', 0, 0, tiled=True)  7.48 us
    pallas_call x1, Pallas kernels, fit_and_detect(): pl.pallas_call(functools.partial(beam_kernel, blocks), out_shape=(jax.Sha...  6.49 us
    all_to_all x1, waiting for transfers between devices, body(): cal = lax.all_to_all(packed, 'chan', 0, 0, tiled=True)  2.57 us
    pallas_call x1, Pallas kernels, pack(): pl.pallas_call(pack_kernel, out_shape=jax.ShapeDtypeStruct((devices, 16,...  1.47 us
    unnamed x1, local copies, waits for them, and re-layouts  0.88 us
  transfers between devices with their start and end apart: 1, of which 1 were waited for; matrix products, arithmetic and copies ran while one was open for 0% of the time, Pallas kernels for 18%

profile of v2, /device:TPU:0, one launch (start us, length us, event | category | flops | bytes accessed | tf_op | source)
XLA Modules:
  0.0 40.6 jit_solution(16137354491444160735)
XLA Ops:
  0.6 1.5 %pack.1 = f32[16,16,256]{2,1,0:T(8,128)} custom-call(f32[4,512]{1,0:T(4,128)} %bitcast.10, f32[2,512]{1,0:T(2,128)} %bitcast.11, s32[1,512]{1,0:T(1,128)} %flag_hbm.1), custom_call_target="tpu_custom_call" | custom-call | tf_op jit(solution)/shard_map/pack/pallas_call | solution.py:67
  2.1 7.5 %all-to-all-start = ((f32[16,16,256]{2,1,0:T(8,128)}), f32[16,16,256]{2,1,0:T(8,128)}, u32[]{:S(2)}, u32[]{:S(2)}) async-start(f32[16,16,256]{2,1,0:T(8,128)} %pack.1), calls=%async_computation | async-start | bytes 524288 | tf_op jit(solution)/shard_map/all_to_all | solution.py:352
  9.6 7.5 %phasors.1 = (f32[2,1024,512]{2,1,0:T(8,128)}, bf16[2,1024,512]{2,1,0:T(8,128)(2,1)}) custom-call(bf16[2,256,1024]{2,1,0:T(8,128)(2,1)} %bitcast.7, f32[2,512]{1,0:T(2,128)} %pos_hbm.1, f32[2,1024]{1,0:T(2,128)} %dir_hbm.1, s32[1,1024]{1,0:T(1,128)} %bitcast.12), custom_call_target="tpu_custom_call" | custom-call | flops 31457280 | bytes 8388608 | tf_op jit(solution)/shard_map/phasors/pallas_call | solution.py:185
  17.1 2.6 %all-to-all-done.cal_ref = f32[16,16,256]{2,1,0:T(8,128)} async-done(((f32[16,16,256]{2,1,0:T(8,128)}), f32[16,16,256]{2,1,0:T(8,128)}, u32[]{:S(2)}, u32[]{:S(2)}) %all-to-all-start) | async-done | bytes 262176 | tf_op jit(solution)/shard_map/all_to_all | solution.py:352
  19.7 6.5 %beams.1 = (bf16[1024,128]{1,0:T(8,128)(2,1)}, f32[4,512]{1,0:T(4,128)}) custom-call(f32[16,16,256]{2,1,0:T(8,128)} %all-to-all-done.cal_ref, f32[2,1024,512]{2,1,0:T(8,128)} %get-tuple-element.6.phase_hbm, bf16[2,1024,512]{2,1,0:T(8,128)(2,1)} %get-tuple-element.7.rhs_hbm), custom_call_target="tpu_custom_call" | custom-call | tf_op jit(solution)/shard_map/beams/pallas_call | solution.py:328
  26.2 13.5 %all_to_all.14 = bf16[16,64,128]{2,1,0:T(8,128)(2,1)S(1)} all-to-all(bf16[16,64,128]{2,1,0:T(8,128)(2,1)} %bitcast.9), channel_id=1, replica_groups=mesh['group'=2,'chan'=16] {'chan'}, dimensions={0} | all-to-all | bytes 524288 | tf_op jit(solution)/shard_map/all_to_all | solution.py:355
  39.7 0.9 %copy.10 = bf16[64,16,128]{2,1,0:T(8,128)(2,1)} copy(bf16[64,16,128]{2,0,1:T(8,128)(2,1)S(1)} %bitcast.8) | data formatting | bytes 524288
Async XLA Ops:
  2.1 17.6 %all-to-all-start = ((f32[16,16,256]{2,1,0:T(8,128)}), f32[16,16,256]{2,1,0:T(8,128)}, u32[]{:S(2)}, u32[]{:S(2)}) async-start(f32[16,16,256]{2,1,0:T(8,128)} %pack.1), calls=%async_computation | async-start | bytes 524288 | tf_op jit(solution)/shard_map/all_to_all | solution.py:352

commit v3 on v2

--- a/solution.py
+++ b/solution.py
@@ -13,6 +13,7 @@
 PENALTY = 2.0
 RIDGE = 1.0
 MIB = 1 << 20
+LANES = 128
 GRANT = 67_000_000
 
 
@@ -57,7 +58,7 @@
     weight4 = jnp.concatenate([weight[0:1], weight[0:1], weight[1:2], weight[1:2]], 0)
     block = jnp.concatenate(
         [num[:, :half], num[:, half:], weight4[:, :half], weight4[:, half:]], 0
-    )
+    ).astype(out_ref.dtype)
     for peer in range(out_ref.shape[0]):
         out_ref[peer] = block
 
@@ -66,7 +67,7 @@
     stations = cal_num.shape[1]
     return pl.pallas_call(
         pack_kernel,
-        out_shape=jax.ShapeDtypeStruct((devices, 16, stations // 2), jnp.float32),
+        out_shape=jax.ShapeDtypeStruct((devices, 16, stations // 2), jnp.bfloat16),
         in_specs=[HBM_SPEC] * 3,
         out_specs=VMEM_SPEC,
         scratch_shapes=[
@@ -98,6 +99,12 @@
     for c in coefficients[-2::-1]:
         value = value * x + c
     return value
+
+
+def thirds(x):
+    high = x.astype(jnp.bfloat16).astype(jnp.float32)
+    middle = (x - high).astype(jnp.bfloat16).astype(jnp.float32)
+    return [high, middle, x - high - middle]
 
 
 def phasor_kernel(
@@ -119,42 +126,29 @@
     for copy in incoming[:3]:
         copy.wait()
 
-    d = dir_ref[...]
-    high = d.astype(jnp.bfloat16).astype(jnp.float32)
-    middle = (d - high).astype(jnp.bfloat16).astype(jnp.float32)
-    low = d - high - middle
-    parts = jnp.concatenate([high, middle, low, jnp.zeros_like(d)], 0).astype(jnp.bfloat16)
+    parts = jnp.concatenate(thirds(dir_ref[...]) + [jnp.zeros_like(dir_ref[...])], 0)
+    groups = table // LANES
+    stack = jnp.concatenate([parts[:, g * LANES : (g + 1) * LANES] for g in range(groups)], 0)
+    point = point_ref[...]
     hot = (
-        (lax.broadcasted_iota(jnp.int32, (table, beams), 0) == point_ref[...])
+        (lax.broadcasted_iota(jnp.int32, (LANES, beams), 0) == (point & (LANES - 1)))
         .astype(jnp.float32)
         .astype(jnp.bfloat16)
     )
-    found = jnp.dot(parts, hot, preferred_element_type=jnp.float32)
-    exact = found[0:2] + found[2:4] + found[4:6]
-    dirs[...] = jnp.transpose(jnp.concatenate([exact] * 4, 0))
-
-    sine_c, cosine_c = fit_polynomials()
-    east = pos_ref[0:1, :] * ratio
-    north = pos_ref[1:2, :] * ratio
-    magic = 12582912.0
-    per_block = beams // blocks
+    spots = jnp.dot(stack.astype(jnp.bfloat16), hot, preferred_element_type=jnp.float32)
+    group = point // LANES
+    found = jnp.where(group == 0, spots[0:8], 0.0)
+    for g in range(1, groups):
+        found = found + jnp.where(group == g, spots[8 * g : 8 * g + 8], 0.0)
+    dirs[...] = jnp.transpose(jnp.concatenate([found] * 4, 0)).astype(jnp.bfloat16)
+    place = pos_ref[...] * ratio
+    places = jnp.concatenate(
+        [jnp.concatenate([third] * 3 + [jnp.zeros_like(third)], 0) for third in thirds(place)]
+        + [jnp.zeros((8, stations), jnp.float32)],
+        0,
+    ).astype(jnp.bfloat16)
+
     outgoing = []
-    for block in range(blocks):
-
-        @pl.loop(0, per_block // rows, unroll=2)
-        def _(step):
-            at = pl.ds(pl.multiple_of(block * per_block + step * rows, rows), rows)
-            turns = dirs[at, 0:1] * east + dirs[at, 1:2] * north
-            x = turns - ((turns + magic) - magic)
-            square = x * x
-            s = x * horner(sine_c, square)
-            c = horner(cosine_c, square)
-            phase_ref[0, at, :] = 1.0 - s * s
-            phase_ref[1, at, :] = s * c
-
-        part = pl.ds(block * per_block, per_block)
-        outgoing.append(start(phase_ref.at[:, part], phase_hbm.at[:, part], out_sems.at[block]))
-
     incoming[3].wait()
     half = samples // 2
     row = lax.broadcasted_iota(jnp.int32, (samples, samples), 0)
@@ -165,12 +159,24 @@
         turned = lax.dot_general(
             volts_ref[polar], spread, (((0,), (0,)), ((), ())), preferred_element_type=jnp.float32
         )
-        real, imag = turned[:stations], turned[stations:]
-        rhs_ref[polar, :stations, :samples] = real.astype(jnp.bfloat16)
-        rhs_ref[polar, stations:, :samples] = (-imag).astype(jnp.bfloat16)
-        rhs_ref[polar, :stations, samples:] = imag.astype(jnp.bfloat16)
-        rhs_ref[polar, stations:, samples:] = real.astype(jnp.bfloat16)
+        rhs_ref[polar] = turned.astype(jnp.bfloat16)
         outgoing.append(start(rhs_ref.at[polar], rhs_hbm.at[polar], out_sems.at[blocks + polar]))
+    sine_c, cosine_c = fit_polynomials()
+    magic = 12582912.0
+    per_block = beams // blocks
+    for block in range(blocks):
+        for step in range(per_block // rows):
+            at = pl.ds(block * per_block + step * rows, rows)
+            turns = jnp.dot(dirs[at, :], places, preferred_element_type=jnp.float32)
+            x = turns - ((turns + magic) - magic)
+            square = x * x
+            s = x * horner(sine_c, square)
+            c = horner(cosine_c, square)
+            phase_ref[0, at, :] = 1.0 - s * s
+            phase_ref[1, at, :] = s * c
+        part = pl.ds(block * per_block, per_block)
+        outgoing.append(start(phase_ref.at[:, part], phase_hbm.at[:, part], out_sems.at[block]))
+
     for copy in outgoing:
         copy.wait()
 
@@ -179,11 +185,11 @@
     beams = pointing.shape[1]
     stations = positions.shape[1]
     samples = volts.shape[1]
-    blocks = 4
+    blocks = 8
     phase = (2, beams, stations)
-    rhs = (2, 2 * stations, 2 * samples)
+    rhs = (2, 2 * stations, samples)
     return pl.pallas_call(
-        functools.partial(phasor_kernel, 16, blocks, total),
+        functools.partial(phasor_kernel, 64, blocks, total),
         out_shape=(
             jax.ShapeDtypeStruct(phase, jnp.float32),
             jax.ShapeDtypeStruct(rhs, jnp.bfloat16),
@@ -197,11 +203,11 @@
             pltpu.VMEM(pointing.shape, jnp.int32),
             pltpu.VMEM(phase, jnp.float32),
             pltpu.VMEM(rhs, jnp.bfloat16),
-            pltpu.VMEM((beams, 8), jnp.float32),
+            pltpu.VMEM((beams, 32), jnp.bfloat16),
             pltpu.SemaphoreType.DMA((4,)),
             pltpu.SemaphoreType.DMA((blocks + 2,)),
         ],
-        compiler_params=pltpu.CompilerParams(vmem_limit_bytes=GRANT),
+        compiler_params=pltpu.CompilerParams(vmem_limit_bytes=GRANT - 2 * MIB),
         cost_estimate=pl.CostEstimate(
             flops=60 * beams * stations, bytes_accessed=8 * MIB, transcendentals=0
         ),
@@ -234,75 +240,94 @@
     return total
 
 
-def solve(cal_ref, target, gain, mask_ref, dual, local):
+def solve(cal_ref, target, keep, lean, history):
     total = cal_ref.shape[0]
     half = cal_ref.shape[2]
-    rows = [[float(v) for v in line] for line in basis_table(total)]
+    table = basis_table(total)
+    pairs = [(c, total - 1 - c, [float(v) for v in table[c]]) for c in range(total // 2)]
+
+    def gather_sums(sums, first, second, line):
+        even, odd = first + second, first - second
+        terms = (even, line[1] * odd, line[2] * even, line[3] * odd)
+        return [t if s is None else s + t for s, t in zip(sums, terms)]
 
     gram = [[None] * ORDER for _ in range(ORDER)]
-    for c in range(total):
-        weight = cal_ref[c, 8:16, :]
-        mask = jnp.where(weight > 0.0, 1.0, 0.0)
-        inverse = mask / (weight + PENALTY)
-        target[c] = cal_ref[c, 0:8, :] * inverse
-        gain[c] = PENALTY * inverse
-        mask_ref[c] = mask
-        dual[c] = jnp.zeros_like(mask)
-        local[c] = jnp.zeros_like(mask)
+    sums = [None] * ORDER
+    for first, second, line in pairs:
+        masks, values = [], []
+        for c in (first, second):
+            block = cal_ref[c].astype(jnp.float32)
+            weight = block[8:16]
+            mask = jnp.where(weight > 0.0, 1.0, 0.0)
+            inverse = 1.0 / (weight + PENALTY)
+            gain = mask * (PENALTY * inverse)
+            value = block[0:8] * inverse
+            target[c] = value
+            history[c] = value
+            keep[c] = mask - gain
+            lean[c] = 2.0 * gain - mask
+            masks.append(mask)
+            values.append(value)
+        sums = gather_sums(sums, *values, line)
+        even, odd = masks[0] + masks[1], masks[0] - masks[1]
         for k in range(ORDER):
             for j in range(k, ORDER):
-                term = mask * (rows[c][k] * rows[c][j])
+                term = (even if (k + j) % 2 == 0 else odd) * (line[k] * line[j])
                 gram[k][j] = term if gram[k][j] is None else gram[k][j] + term
     for k in range(ORDER):
         gram[k][k] = gram[k][k] + RIDGE
         for j in range(k):
             gram[k][j] = gram[j][k]
     inverse = invert_small(gram)
+    coefficients = tuple(combine(inverse[k], sums) for k in range(ORDER))
 
     def sweep(_, coefficients):
         sums = [None] * ORDER
-        for c in range(total):
-            fitted = combine(rows[c], coefficients)
-            d = dual[c] + (local[c] - mask_ref[c] * fitted)
-            new = target[c] + gain[c] * (fitted - d)
-            dual[c] = d
-            local[c] = new
-            u = new + d
-            for k in range(ORDER):
-                term = u if rows[c][k] == 1.0 else rows[c][k] * u
-                sums[k] = term if sums[k] is None else sums[k] + term
+        for first, second, line in pairs:
+            even = coefficients[0] + line[2] * coefficients[2]
+            odd = line[1] * coefficients[1] + line[3] * coefficients[3]
+            values = []
+            for c, fitted in ((first, even + odd), (second, even - odd)):
+                u = (target[c] + keep[c] * history[c]) + lean[c] * fitted
+                history[c] = u
+                values.append(u)
+            sums = gather_sums(sums, *values, line)
         return tuple(combine(inverse[k], sums) for k in range(ORDER))
 
-    zero = jnp.zeros((8, half), jnp.float32)
-    coefficients = lax.fori_loop(0, ITERS, sweep, (zero,) * ORDER)
+    coefficients = lax.fori_loop(1, ITERS, sweep, coefficients)
     channel = lax.axis_index("chan").astype(jnp.float32)
     place = 2.0 * (channel + 0.5) / total - 1.0
     return combine(legendre(place), coefficients)
 
 
 def beam_kernel(
-    blocks, cal_ref, phase_hbm, rhs_hbm, out_ref, fitted_ref,
-    phase_ref, rhs_ref, target, gain, mask_ref, dual, local, sems,
+    blocks, cal_hbm, phase_hbm, rhs_hbm, out_ref, fitted_ref,
+    cal_ref, phase_ref, rhs_ref, target, keep, lean, history, sems,
 ):
     stations = phase_ref.shape[2]
-    samples = rhs_ref.shape[2] // 2
-    half = samples // 2
+    half = rhs_ref.shape[2] // 2
     per_block = phase_ref.shape[1] // blocks
-    rhs_copy = start(rhs_hbm, rhs_ref, sems.at[0])
-    phase_copies = []
-    for block in range(blocks):
+    cal_copy = start(cal_hbm, cal_ref, sems.at[0])
+    rhs_copy = start(rhs_hbm, rhs_ref, sems.at[1])
+
+    def fetch(block):
         part = pl.ds(block * per_block, per_block)
-        phase_copies.append(start(phase_hbm.at[:, part], phase_ref.at[:, part], sems.at[1 + block]))
-
-    fitted = solve(cal_ref, target, gain, mask_ref, dual, local)
+        return start(phase_hbm.at[:, part], phase_ref.at[:, part], sems.at[2 + block])
+
+    copies = [fetch(0)]
+    cal_copy.wait()
+    fitted = solve(cal_ref, target, keep, lean, history)
     fitted_ref[:, : stations // 2] = fitted[0:4]
     fitted_ref[:, stations // 2 :] = fitted[4:8]
-    dense = fitted * (mask_ref[lax.axis_index("chan")] * stations ** (-0.5))
+    own = cal_ref[lax.axis_index("chan")].astype(jnp.float32)[8:16]
+    dense = fitted * jnp.where(own > 0.0, stations ** (-0.5), 0.0)
     gains = jnp.concatenate([dense[0:4], dense[4:8]], 1)
     rhs_copy.wait()
     for block in range(blocks):
         part = pl.ds(block * per_block, per_block)
-        phase_copies[block].wait()
+        copies[block].wait()
+        if block == 0:
+            copies += [fetch(later) for later in range(1, blocks)]
         cosine = phase_ref[0, part]
         sine = phase_ref[1, part]
         power = None
@@ -311,10 +336,12 @@
             im = gains[2 * polar + 1 : 2 * polar + 2]
             w_re = (re * cosine - im * sine).astype(jnp.bfloat16)
             w_im = (-(re * sine + im * cosine)).astype(jnp.bfloat16)
-            lhs = jnp.concatenate([w_re, w_im], 1)
+            lhs = jnp.concatenate(
+                [jnp.concatenate([w_re, -w_im], 1), jnp.concatenate([w_im, w_re], 1)], 0
+            )
             y = jnp.dot(lhs, rhs_ref[polar], preferred_element_type=jnp.float32)
             y = y * y
-            y = y[:, :samples] + y[:, samples:]
+            y = y[:per_block] + y[per_block:]
             power = y if power is None else power + y
         out_ref[part, :] = ((power[:, :half] + power[:, half:]) * 0.5).astype(jnp.bfloat16)
 
@@ -322,8 +349,8 @@
 def fit_and_detect(cal, phase, rhs):
     total, _, half_stations = cal.shape
     _, beams, stations = phase.shape
-    samples = rhs.shape[2] // 2
-    blocks = 4
+    samples = rhs.shape[2]
+    blocks = 2
     state = pltpu.VMEM((total, 8, half_stations), jnp.float32)
     return pl.pallas_call(
         functools.partial(beam_kernel, blocks),
@@ -331,15 +358,16 @@
             jax.ShapeDtypeStruct((beams, samples // 2), jnp.bfloat16),
             jax.ShapeDtypeStruct((4, stations), jnp.float32),
         ),
-        in_specs=[VMEM_SPEC, HBM_SPEC, HBM_SPEC],
+        in_specs=[HBM_SPEC] * 3,
         out_specs=(VMEM_SPEC, VMEM_SPEC),
         scratch_shapes=[
+            pltpu.VMEM(cal.shape, cal.dtype),
             pltpu.VMEM(phase.shape, jnp.float32),
             pltpu.VMEM(rhs.shape, jnp.bfloat16),
         ]
-        + [state] * 5
-        + [pltpu.SemaphoreType.DMA((1 + blocks,))],
-        compiler_params=pltpu.CompilerParams(vmem_limit_bytes=GRANT - MIB),
+        + [state] * 4
+        + [pltpu.SemaphoreType.DMA((2 + blocks,))],
+        compiler_params=pltpu.CompilerParams(vmem_limit_bytes=GRANT - 11 * MIB),
         name="beams",
     )(cal, phase, rhs)
 

time: 41.1 us -> 36.2 us (0.88)
  Pallas kernels: 15.5 us -> 10.9 us
  blocking collectives: 13.5 us -> 12.6 us
  waiting for transfers between devices: 2.57 us -> 3.33 us
    pallas_call x1, Pallas kernels: 7.49 us -> 4.56 us  [phasors(): pl.pallas_call(functools.partial(phasor_kernel, 64, blocks, total), out_s...]
    pallas_call x1, Pallas kernels: 6.49 us -> 4.96 us  [fit_and_detect(): pl.pallas_call(functools.partial(beam_kernel, blocks), out_shape=(jax.Sha...]
    all_to_all x1, blocking collectives: 13.5 us -> 12.6 us  [body(): moved = lax.all_to_all(power, 'chan', 0, 0, tiled=True)]
    all_to_all x1, waiting for transfers between devices: 2.57 us -> 3.33 us  [body(): cal = lax.all_to_all(packed, 'chan', 0, 0, tiled=True)]
  transfers between devices with their start and end apart: 1 -> 1, of which waited for: 1 -> 1; matrix products, arithmetic and copies ran while one was open for 0% -> 0% of each run, Pallas kernels for 18% -> 13%
where the time goes in v3:
time: 36.2 us; the launch traced here: 35.8 us
  blocking collectives  12.6 us (35%)
  Pallas kernels  10.9 us (30%)
  starting transfers between devices  7.43 us (21%)
  waiting for transfers between devices  3.33 us (9%)
  local copies, waits for them, and re-layouts  0.88 us (2%)
  between operations  0.66 us (2%)
    all_to_all x1, blocking collectives, body(): moved = lax.all_to_all(power, 'chan', 0, 0, tiled=True)  12.6 us
    all_to_all x1, starting transfers between devices, body(): cal = lax.all_to_all(packed, 'chan', 0, 0, tiled=True)  7.43 us
    pallas_call x1, Pallas kernels, fit_and_detect(): pl.pallas_call(functools.partial(beam_kernel, blocks), out_shape=(jax.Sha...  4.96 us
    pallas_call x1, Pallas kernels, phasors(): pl.pallas_call(functools.partial(phasor_kernel, 64, blocks, total), out_s...  4.56 us
    all_to_all x1, waiting for transfers between devices, body(): cal = lax.all_to_all(packed, 'chan', 0, 0, tiled=True)  3.33 us
    pallas_call x1, Pallas kernels, pack(): pl.pallas_call(pack_kernel, out_shape=jax.ShapeDtypeStruct((devices, 16,...  1.41 us
    unnamed x1, local copies, waits for them, and re-layouts  0.88 us
  transfers between devices with their start and end apart: 1, of which 1 were waited for; matrix products, arithmetic and copies ran while one was open for 0% of the time, Pallas kernels for 13%

profile of v3, /device:TPU:0, one launch (start us, length us, event | category | flops | bytes accessed | tf_op | source)
XLA Modules:
  0.0 35.8 jit_solution(2200089233466776336)
XLA Ops:
  0.6 1.4 %pack.1 = bf16[16,16,256]{2,1,0:T(8,128)(2,1)} custom-call(f32[4,512]{1,0:T(4,128)} %bitcast.10, f32[2,512]{1,0:T(2,128)} %bitcast.12, s32[1,512]{1,0:T(1,128)} %flag_hbm.1), custom_call_target="tpu_custom_call" | custom-call | tf_op jit(solution)/shard_map/pack/pallas_call | solution.py:68
  2.0 7.4 %all-to-all-start = ((bf16[16,16,256]{2,1,0:T(8,128)(2,1)}), bf16[16,16,256]{2,1,0:T(8,128)(2,1)S(1)}, u32[]{:S(2)}, u32[]{:S(2)}) async-start(bf16[16,16,256]{2,1,0:T(8,128)(2,1)} %pack.1), calls=%async_computation | async-start | bytes 262144 | tf_op jit(solution)/shard_map/all_to_all | solution.py:380
  9.5 4.6 %phasors.1 = (f32[2,1024,512]{2,1,0:T(8,128)}, bf16[2,1024,256]{2,1,0:T(8,128)(2,1)}) custom-call(bf16[2,256,1024]{2,1,0:T(8,128)(2,1)} %bitcast.8, f32[2,512]{1,0:T(2,128)} %pos_hbm.1, f32[2,1024]{1,0:T(2,128)} %dir_hbm.1, s32[1,1024]{1,0:T(1,128)} %bitcast.11), custom_call_target="tpu_custom_call" | custom-call | flops 31457280 | bytes 8388608 | tf_op jit(solution)/shard_map/phasors/pallas_call | solution.py:191
  14.1 3.3 %all-to-all-done.cal_hbm = bf16[16,16,256]{2,1,0:T(8,128)(2,1)S(1)} async-done(((bf16[16,16,256]{2,1,0:T(8,128)(2,1)}), bf16[16,16,256]{2,1,0:T(8,128)(2,1)S(1)}, u32[]{:S(2)}, u32[]{:S(2)}) %all-to-all-start) | async-done | bytes 131104 | tf_op jit(solution)/shard_map/all_to_all | solution.py:380
  17.4 5.0 %beams.1 = (bf16[1024,128]{1,0:T(8,128)(2,1)S(1)}, f32[4,512]{1,0:T(4,128)}) custom-call(bf16[16,16,256]{2,1,0:T(8,128)(2,1)S(1)} %all-to-all-done.cal_hbm, f32[2,1024,512]{2,1,0:T(8,128)} %get-tuple-element.6.phase_hbm, bf16[2,1024,256]{2,1,0:T(8,128)(2,1)} %get-tuple-element.7.rhs_hbm), custom_call_target="tpu_custom_call" | custom-call | tf_op jit(solution)/shard_map/beams/pallas_call | solution.py:355
  22.4 12.6 %all_to_all.14 = bf16[16,64,128]{2,1,0:T(8,128)(2,1)S(1)} all-to-all(bf16[16,64,128]{2,1,0:T(8,128)(2,1)S(1)} %bitcast.7), channel_id=1, replica_groups=mesh['group'=2,'chan'=16] {'chan'}, dimensions={0} | all-to-all | bytes 524288 | tf_op jit(solution)/shard_map/all_to_all | solution.py:383
  35.0 0.9 %copy.10 = bf16[64,16,128]{2,1,0:T(8,128)(2,1)} copy(bf16[64,16,128]{2,0,1:T(8,128)(2,1)S(1)} %bitcast.9) | data formatting | bytes 524288
Async XLA Ops:
  2.0 15.3 %all-to-all-start = ((bf16[16,16,256]{2,1,0:T(8,128)(2,1)}), bf16[16,16,256]{2,1,0:T(8,128)(2,1)S(1)}, u32[]{:S(2)}, u32[]{:S(2)}) async-start(bf16[16,16,256]{2,1,0:T(8,128)(2,1)} %pack.1), calls=%async_computation | async-start | bytes 262144 | tf_op jit(solution)/shard_map/all_to_all | solution.py:380

commit v4 on v3

--- a/solution.py
+++ b/solution.py
@@ -41,6 +41,25 @@
     copy = pltpu.make_async_copy(source, target, semaphore)
     copy.start()
     return copy
+
+
+NUM_MOST = 6.0
+WEIGHT_MOST = 5.0
+LEVELS = 32767.0
+STEPS = 14
+
+
+def stacked(x):
+    half = x.shape[1] // 2
+    return jnp.concatenate([x[:, :half], x[:, half:]], 0)
+
+
+def even_rows(x):
+    return lax.broadcasted_iota(jnp.int32, x.shape, 0) % 2 == 0
+
+
+def beside(x, even):
+    return jnp.where(even, pltpu.roll(x, 7, 0), pltpu.roll(x, 1, 0))
 
 
 def pack_kernel(num_hbm, weight_hbm, flag_hbm, out_ref, num_ref, weight_ref, flag_ref, sems):
@@ -51,23 +70,42 @@
     ]
     for copy in copies:
         copy.wait()
-    half = num_ref.shape[1] // 2
     mask = flag_ref[...].astype(jnp.float32)
-    num = num_ref[...] * mask
+    num = stacked(num_ref[...] * mask)
     weight = weight_ref[...] * mask
-    weight4 = jnp.concatenate([weight[0:1], weight[0:1], weight[1:2], weight[1:2]], 0)
-    block = jnp.concatenate(
-        [num[:, :half], num[:, half:], weight4[:, :half], weight4[:, half:]], 0
-    ).astype(out_ref.dtype)
+    weight = stacked(jnp.concatenate([weight[0:1], weight[0:1], weight[1:2], weight[1:2]], 0))
+    even = even_rows(num)
+    size = jnp.abs(num)
+    size = jnp.maximum(size, beside(size, even))
+    scale = jnp.ones_like(size)
+    inverse = jnp.ones_like(size)
+    for power in range(1, STEPS + 1):
+        larger = size > NUM_MOST * 2.0 ** (power - 1 - STEPS)
+        scale = jnp.where(larger, 2.0**power, scale)
+        inverse = jnp.where(larger, 2.0**-power, inverse)
+    coded = jnp.round(num * inverse * (LEVELS * 2.0**STEPS / NUM_MOST))
+    coded = jnp.clip(coded, -LEVELS, LEVELS)
+    level = jnp.clip(jnp.round(weight * (LEVELS / WEIGHT_MOST)), 0.0, LEVELS)
+    block = jnp.concatenate([coded, jnp.where(even, level, scale)], 0)
+    block = block.astype(jnp.int32).astype(out_ref.dtype)
     for peer in range(out_ref.shape[0]):
         out_ref[peer] = block
+
+
+def unpack(block):
+    block = block.astype(jnp.int32).astype(jnp.float32)
+    coded, side = block[0:8], block[8:16]
+    even = even_rows(side)
+    weight = jnp.where(even, side, pltpu.roll(side, 1, 0)) * (WEIGHT_MOST / LEVELS)
+    scale = jnp.where(even, pltpu.roll(side, 7, 0), side)
+    return coded * (scale * (NUM_MOST / (LEVELS * 2.0**STEPS))), weight
 
 
 def pack(cal_num, cal_weight, flags, devices):
     stations = cal_num.shape[1]
     return pl.pallas_call(
         pack_kernel,
-        out_shape=jax.ShapeDtypeStruct((devices, 16, stations // 2), jnp.bfloat16),
+        out_shape=jax.ShapeDtypeStruct((devices, 16, stations // 2), jnp.int16),
         in_specs=[HBM_SPEC] * 3,
         out_specs=VMEM_SPEC,
         scratch_shapes=[
@@ -256,12 +294,11 @@
     for first, second, line in pairs:
         masks, values = [], []
         for c in (first, second):
-            block = cal_ref[c].astype(jnp.float32)
-            weight = block[8:16]
+            num, weight = unpack(cal_ref[c])
             mask = jnp.where(weight > 0.0, 1.0, 0.0)
             inverse = 1.0 / (weight + PENALTY)
             gain = mask * (PENALTY * inverse)
-            value = block[0:8] * inverse
+            value = num * inverse
             target[c] = value
             history[c] = value
             keep[c] = mask - gain
@@ -319,7 +356,7 @@
     fitted = solve(cal_ref, target, keep, lean, history)
     fitted_ref[:, : stations // 2] = fitted[0:4]
     fitted_ref[:, stations // 2 :] = fitted[4:8]
-    own = cal_ref[lax.axis_index("chan")].astype(jnp.float32)[8:16]
+    _, own = unpack(cal_ref[lax.axis_index("chan")])
     dense = fitted * jnp.where(own > 0.0, stations ** (-0.5), 0.0)
     gains = jnp.concatenate([dense[0:4], dense[4:8]], 1)
     rhs_copy.wait()

time: 36.2 us -> 36.2 us (level)
  no operation moved by 1% of the time
where the time goes in v4:
time: 36.2 us; the launch traced here: 35.9 us
  blocking collectives  12.6 us (35%)
  Pallas kernels  11 us (30%)
  starting transfers between devices  7.43 us (21%)
  waiting for transfers between devices  3.33 us (9%)
  local copies, waits for them, and re-layouts  0.88 us (2%)
  between operations  0.66 us (2%)
    all_to_all x1, blocking collectives, body(): moved = lax.all_to_all(power, 'chan', 0, 0, tiled=True)  12.6 us
    all_to_all x1, starting transfers between devices, body(): cal = lax.all_to_all(packed, 'chan', 0, 0, tiled=True)  7.43 us
    pallas_call x1, Pallas kernels, fit_and_detect(): pl.pallas_call(functools.partial(beam_kernel, blocks), out_shape=(jax.Sha...  4.96 us
    pallas_call x1, Pallas kernels, phasors(): pl.pallas_call(functools.partial(phasor_kernel, 64, blocks, total), out_s...  4.56 us
    all_to_all x1, waiting for transfers between devices, body(): cal = lax.all_to_all(packed, 'chan', 0, 0, tiled=True)  3.33 us
    pallas_call x1, Pallas kernels, pack(): pl.pallas_call(pack_kernel, out_shape=jax.ShapeDtypeStruct((devices, 16,...  1.43 us
    unnamed x1, local copies, waits for them, and re-layouts  0.88 us
  transfers between devices with their start and end apart: 1, of which 1 were waited for; matrix products, arithmetic and copies ran while one was open for 0% of the time, Pallas kernels for 13%

profile of v4, /device:TPU:0, one launch (start us, length us, event | category | flops | bytes accessed | tf_op | source)
XLA Modules:
  0.0 35.9 jit_solution(14999267017239962585)
XLA Ops:
  0.6 1.4 %pack.1 = s16[16,16,256]{2,1,0:T(8,128)(2,1)} custom-call(f32[4,512]{1,0:T(4,128)} %bitcast.10, f32[2,512]{1,0:T(2,128)} %bitcast.12, s32[1,512]{1,0:T(1,128)} %flag_hbm.1), custom_call_target="tpu_custom_call" | custom-call | tf_op jit(solution)/shard_map/pack/pallas_call | solution.py:106
  2.1 7.4 %all-to-all-start = ((s16[16,16,256]{2,1,0:T(8,128)(2,1)}), s16[16,16,256]{2,1,0:T(8,128)(2,1)S(1)}, u32[]{:S(2)}, u32[]{:S(2)}) async-start(s16[16,16,256]{2,1,0:T(8,128)(2,1)} %pack.1), calls=%async_computation | async-start | bytes 262144 | tf_op jit(solution)/shard_map/all_to_all | solution.py:417
  9.5 4.6 %phasors.1 = (f32[2,1024,512]{2,1,0:T(8,128)}, bf16[2,1024,256]{2,1,0:T(8,128)(2,1)}) custom-call(bf16[2,256,1024]{2,1,0:T(8,128)(2,1)} %bitcast.8, f32[2,512]{1,0:T(2,128)} %pos_hbm.1, f32[2,1024]{1,0:T(2,128)} %dir_hbm.1, s32[1,1024]{1,0:T(1,128)} %bitcast.11), custom_call_target="tpu_custom_call" | custom-call | flops 31457280 | bytes 8388608 | tf_op jit(solution)/shard_map/phasors/pallas_call | solution.py:229
  14.1 3.3 %all-to-all-done.cal_hbm = s16[16,16,256]{2,1,0:T(8,128)(2,1)S(1)} async-done(((s16[16,16,256]{2,1,0:T(8,128)(2,1)}), s16[16,16,256]{2,1,0:T(8,128)(2,1)S(1)}, u32[]{:S(2)}, u32[]{:S(2)}) %all-to-all-start) | async-done | bytes 131104 | tf_op jit(solution)/shard_map/all_to_all | solution.py:417
  17.4 5.0 %beams.1 = (bf16[1024,128]{1,0:T(8,128)(2,1)S(1)}, f32[4,512]{1,0:T(4,128)}) custom-call(s16[16,16,256]{2,1,0:T(8,128)(2,1)S(1)} %all-to-all-done.cal_hbm, f32[2,1024,512]{2,1,0:T(8,128)} %get-tuple-element.6.phase_hbm, bf16[2,1024,256]{2,1,0:T(8,128)(2,1)} %get-tuple-element.7.rhs_hbm), custom_call_target="tpu_custom_call" | custom-call | tf_op jit(solution)/shard_map/beams/pallas_call | solution.py:392
  22.4 12.6 %all_to_all.14 = bf16[16,64,128]{2,1,0:T(8,128)(2,1)S(1)} all-to-all(bf16[16,64,128]{2,1,0:T(8,128)(2,1)S(1)} %bitcast.7), channel_id=1, replica_groups=mesh['group'=2,'chan'=16] {'chan'}, dimensions={0} | all-to-all | bytes 524288 | tf_op jit(solution)/shard_map/all_to_all | solution.py:420
  35.0 0.9 %copy.10 = bf16[64,16,128]{2,1,0:T(8,128)(2,1)} copy(bf16[64,16,128]{2,0,1:T(8,128)(2,1)S(1)} %bitcast.9) | data formatting | bytes 524288
Async XLA Ops:
  2.1 15.3 %all-to-all-start = ((s16[16,16,256]{2,1,0:T(8,128)(2,1)}), s16[16,16,256]{2,1,0:T(8,128)(2,1)S(1)}, u32[]{:S(2)}, u32[]{:S(2)}) async-start(s16[16,16,256]{2,1,0:T(8,128)(2,1)} %pack.1), calls=%async_computation | async-start | bytes 262144 | tf_op jit(solution)/shard_map/all_to_all | solution.py:417

commit v5 on v4

--- a/solution.py
+++ b/solution.py
@@ -338,72 +338,74 @@
 
 
 def beam_kernel(
-    blocks, cal_hbm, phase_hbm, rhs_hbm, out_ref, fitted_ref,
-    cal_ref, phase_ref, rhs_ref, target, keep, lean, history, sems,
+    sizes, splits, cal_ref, phase_hbm, rhs_hbm, out_ref, fitted_ref,
+    phase_ref, rhs_ref, target, keep, lean, history, sems,
 ):
     stations = phase_ref.shape[2]
+    beams = phase_ref.shape[1]
     half = rhs_ref.shape[2] // 2
-    per_block = phase_ref.shape[1] // blocks
-    cal_copy = start(cal_hbm, cal_ref, sems.at[0])
-    rhs_copy = start(rhs_hbm, rhs_ref, sems.at[1])
+    edges = [sum(sizes[:block]) * beams // sum(sizes) for block in range(len(sizes) + 1)]
 
     def fetch(block):
-        part = pl.ds(block * per_block, per_block)
+        part = pl.ds(edges[block], edges[block + 1] - edges[block])
         return start(phase_hbm.at[:, part], phase_ref.at[:, part], sems.at[2 + block])
 
     copies = [fetch(0)]
-    cal_copy.wait()
+    rhs_copies = [start(rhs_hbm.at[p], rhs_ref.at[p], sems.at[p]) for p in range(2)]
+    copies += [fetch(later) for later in range(1, min(2, len(sizes)))]
     fitted = solve(cal_ref, target, keep, lean, history)
     fitted_ref[:, : stations // 2] = fitted[0:4]
     fitted_ref[:, stations // 2 :] = fitted[4:8]
     _, own = unpack(cal_ref[lax.axis_index("chan")])
     dense = fitted * jnp.where(own > 0.0, stations ** (-0.5), 0.0)
     gains = jnp.concatenate([dense[0:4], dense[4:8]], 1)
-    rhs_copy.wait()
-    for block in range(blocks):
-        part = pl.ds(block * per_block, per_block)
-        copies[block].wait()
-        if block == 0:
-            copies += [fetch(later) for later in range(1, blocks)]
-        cosine = phase_ref[0, part]
-        sine = phase_ref[1, part]
-        power = None
-        for polar in range(2):
-            re = gains[2 * polar : 2 * polar + 1]
-            im = gains[2 * polar + 1 : 2 * polar + 2]
-            w_re = (re * cosine - im * sine).astype(jnp.bfloat16)
-            w_im = (-(re * sine + im * cosine)).astype(jnp.bfloat16)
-            lhs = jnp.concatenate(
-                [jnp.concatenate([w_re, -w_im], 1), jnp.concatenate([w_im, w_re], 1)], 0
-            )
-            y = jnp.dot(lhs, rhs_ref[polar], preferred_element_type=jnp.float32)
-            y = y * y
-            y = y[:per_block] + y[per_block:]
-            power = y if power is None else power + y
-        out_ref[part, :] = ((power[:, :half] + power[:, half:]) * 0.5).astype(jnp.bfloat16)
+    for copy in rhs_copies:
+        copy.wait()
+    for group in range(len(sizes)):
+        copies[group].wait()
+        if group == 0:
+            copies += [fetch(later) for later in range(2, len(sizes))]
+        rows = (edges[group + 1] - edges[group]) // splits[group]
+        for block in range(splits[group]):
+            part = pl.ds(edges[group] + block * rows, rows)
+            cosine = phase_ref[0, part]
+            sine = phase_ref[1, part]
+            power = None
+            for polar in range(2):
+                re = gains[2 * polar : 2 * polar + 1]
+                im = gains[2 * polar + 1 : 2 * polar + 2]
+                w_re = (re * cosine - im * sine).astype(jnp.bfloat16)
+                w_im = (-(re * sine + im * cosine)).astype(jnp.bfloat16)
+                lhs = jnp.concatenate(
+                    [jnp.concatenate([w_re, -w_im], 1), jnp.concatenate([w_im, w_re], 1)], 0
+                )
+                y = jnp.dot(lhs, rhs_ref[polar], preferred_element_type=jnp.float32)
+                y = y * y
+                y = y[:rows] + y[rows:]
+                power = y if power is None else power + y
+            out_ref[part, :] = ((power[:, :half] + power[:, half:]) * 0.5).astype(jnp.bfloat16)
 
 
 def fit_and_detect(cal, phase, rhs):
     total, _, half_stations = cal.shape
     _, beams, stations = phase.shape
     samples = rhs.shape[2]
-    blocks = 2
+    sizes, splits = (1, 3, 4), (1, 1, 1)
     state = pltpu.VMEM((total, 8, half_stations), jnp.float32)
     return pl.pallas_call(
-        functools.partial(beam_kernel, blocks),
+        functools.partial(beam_kernel, sizes, splits),
         out_shape=(
             jax.ShapeDtypeStruct((beams, samples // 2), jnp.bfloat16),
             jax.ShapeDtypeStruct((4, stations), jnp.float32),
         ),
-        in_specs=[HBM_SPEC] * 3,
+        in_specs=[VMEM_SPEC, HBM_SPEC, HBM_SPEC],
         out_specs=(VMEM_SPEC, VMEM_SPEC),
         scratch_shapes=[
-            pltpu.VMEM(cal.shape, cal.dtype),
             pltpu.VMEM(phase.shape, jnp.float32),
             pltpu.VMEM(rhs.shape, jnp.bfloat16),
         ]
         + [state] * 4
-        + [pltpu.SemaphoreType.DMA((2 + blocks,))],
+        + [pltpu.SemaphoreType.DMA((2 + len(sizes),))],
         compiler_params=pltpu.CompilerParams(vmem_limit_bytes=GRANT - 11 * MIB),
         name="beams",
     )(cal, phase, rhs)

time: 36.2 us -> 35.7 us (0.986)
  Pallas kernels: 11 us -> 10.4 us
    pallas_call x1, Pallas kernels: 4.96 us -> 4.39 us  [fit_and_detect(): pl.pallas_call(functools.partial(beam_kernel, sizes, splits), out_shape=(...]
where the time goes in v5:
time: 35.7 us; the launch traced here: 35.3 us
  blocking collectives  12.6 us (35%)
  Pallas kernels  10.4 us (29%)
  starting transfers between devices  7.43 us (21%)
  waiting for transfers between devices  3.33 us (9%)
  local copies, waits for them, and re-layouts  0.88 us (2%)
  between operations  0.66 us (2%)
    all_to_all x1, blocking collectives, body(): moved = lax.all_to_all(power, 'chan', 0, 0, tiled=True)  12.6 us
    all_to_all x1, starting transfers between devices, body(): cal = lax.all_to_all(packed, 'chan', 0, 0, tiled=True)  7.43 us
    pallas_call x1, Pallas kernels, phasors(): pl.pallas_call(functools.partial(phasor_kernel, 64, blocks, total), out_s...  4.56 us
    pallas_call x1, Pallas kernels, fit_and_detect(): pl.pallas_call(functools.partial(beam_kernel, sizes, splits), out_shape=(...  4.39 us
    all_to_all x1, waiting for transfers between devices, body(): cal = lax.all_to_all(packed, 'chan', 0, 0, tiled=True)  3.33 us
    pallas_call x1, Pallas kernels, pack(): pl.pallas_call(pack_kernel, out_shape=jax.ShapeDtypeStruct((devices, 16,...  1.43 us
    unnamed x1, local copies, waits for them, and re-layouts  0.88 us
  transfers between devices with their start and end apart: 1, of which 1 were waited for; matrix products, arithmetic and copies ran while one was open for 0% of the time, Pallas kernels for 13%

profile of v5, /device:TPU:0, one launch (start us, length us, event | category | flops | bytes accessed | tf_op | source)
XLA Modules:
  0.0 35.3 jit_solution(17345193992930203154)
XLA Ops:
  0.6 1.4 %pack.1 = s16[16,16,256]{2,1,0:T(8,128)(2,1)} custom-call(f32[4,512]{1,0:T(4,128)} %bitcast.10, f32[2,512]{1,0:T(2,128)} %bitcast.12, s32[1,512]{1,0:T(1,128)} %flag_hbm.1), custom_call_target="tpu_custom_call" | custom-call | tf_op jit(solution)/shard_map/pack/pallas_call | solution.py:106
  2.1 7.4 %all-to-all-start = ((s16[16,16,256]{2,1,0:T(8,128)(2,1)}), s16[16,16,256]{2,1,0:T(8,128)(2,1)S(1)}, u32[]{:S(2)}, u32[]{:S(2)}) async-start(s16[16,16,256]{2,1,0:T(8,128)(2,1)} %pack.1), calls=%async_computation | async-start | bytes 262144 | tf_op jit(solution)/shard_map/all_to_all | solution.py:419
  9.5 4.6 %phasors.1 = (f32[2,1024,512]{2,1,0:T(8,128)}, bf16[2,1024,256]{2,1,0:T(8,128)(2,1)}) custom-call(bf16[2,256,1024]{2,1,0:T(8,128)(2,1)} %bitcast.8, f32[2,512]{1,0:T(2,128)} %pos_hbm.1, f32[2,1024]{1,0:T(2,128)} %dir_hbm.1, s32[1,1024]{1,0:T(1,128)} %bitcast.11), custom_call_target="tpu_custom_call" | custom-call | flops 31457280 | bytes 8388608 | tf_op jit(solution)/shard_map/phasors/pallas_call | solution.py:229
  14.1 3.3 %all-to-all-done.cal_ref = s16[16,16,256]{2,1,0:T(8,128)(2,1)S(1)} async-done(((s16[16,16,256]{2,1,0:T(8,128)(2,1)}), s16[16,16,256]{2,1,0:T(8,128)(2,1)S(1)}, u32[]{:S(2)}, u32[]{:S(2)}) %all-to-all-start) | async-done | bytes 131104 | tf_op jit(solution)/shard_map/all_to_all | solution.py:419
  17.4 4.4 %beams.1 = (bf16[1024,128]{1,0:T(8,128)(2,1)S(1)}, f32[4,512]{1,0:T(4,128)}) custom-call(s16[16,16,256]{2,1,0:T(8,128)(2,1)S(1)} %all-to-all-done.cal_ref, f32[2,1024,512]{2,1,0:T(8,128)} %get-tuple-element.6.phase_hbm, bf16[2,1024,256]{2,1,0:T(8,128)(2,1)} %get-tuple-element.7.rhs_hbm), custom_call_target="tpu_custom_call" | custom-call | tf_op jit(solution)/shard_map/beams/pallas_call | solution.py:395
  21.8 12.6 %all_to_all.14 = bf16[16,64,128]{2,1,0:T(8,128)(2,1)S(1)} all-to-all(bf16[16,64,128]{2,1,0:T(8,128)(2,1)S(1)} %bitcast.7), channel_id=1, replica_groups=mesh['group'=2,'chan'=16] {'chan'}, dimensions={0} | all-to-all | bytes 524288 | tf_op jit(solution)/shard_map/all_to_all | solution.py:422
  34.4 0.9 %copy.10 = bf16[64,16,128]{2,1,0:T(8,128)(2,1)} copy(bf16[64,16,128]{2,0,1:T(8,128)(2,1)S(1)} %bitcast.9) | data formatting | bytes 524288
Async XLA Ops:
  2.1 15.3 %all-to-all-start = ((s16[16,16,256]{2,1,0:T(8,128)(2,1)}), s16[16,16,256]{2,1,0:T(8,128)(2,1)S(1)}, u32[]{:S(2)}, u32[]{:S(2)}) async-start(s16[16,16,256]{2,1,0:T(8,128)(2,1)} %pack.1), calls=%async_computation | async-start | bytes 262144 | tf_op jit(solution)/shard_map/all_to_all | solution.py:419

commit v6 on v5

--- a/solution.py
+++ b/solution.py
@@ -14,6 +14,8 @@
 RIDGE = 1.0
 MIB = 1 << 20
 LANES = 128
+NEAR = 4
+SPLITS = 1
 GRANT = 67_000_000
 
 
@@ -35,6 +37,10 @@
 
 HBM_SPEC = pl.BlockSpec(memory_space=pltpu.HBM)
 VMEM_SPEC = pl.BlockSpec(memory_space=pltpu.VMEM)
+
+
+def in_hbm(x):
+    return pltpu.with_memory_space_constraint(x, pltpu.HBM)
 
 
 def start(source, target, semaphore):
@@ -146,8 +152,8 @@
 
 
 def phasor_kernel(
-    rows, blocks, total, volts_hbm, pos_hbm, dir_hbm, point_hbm, phase_hbm, rhs_hbm,
-    volts_ref, pos_ref, dir_ref, point_ref, phase_ref, rhs_ref, dirs, sems, out_sems,
+    rows, blocks, total, volts_hbm, pos_hbm, dir_hbm, point_hbm, near_ref, far_hbm, rhs_ref,
+    volts_ref, pos_ref, dir_ref, point_ref, far_ref, dirs, sems, out_sems,
 ):
     incoming = [
         start(point_hbm, point_ref, sems.at[0]),
@@ -198,23 +204,30 @@
             volts_ref[polar], spread, (((0,), (0,)), ((), ())), preferred_element_type=jnp.float32
         )
         rhs_ref[polar] = turned.astype(jnp.bfloat16)
-        outgoing.append(start(rhs_ref.at[polar], rhs_hbm.at[polar], out_sems.at[blocks + polar]))
     sine_c, cosine_c = fit_polynomials()
-    magic = 12582912.0
-    per_block = beams // blocks
-    for block in range(blocks):
-        for step in range(per_block // rows):
-            at = pl.ds(block * per_block + step * rows, rows)
-            turns = jnp.dot(dirs[at, :], places, preferred_element_type=jnp.float32)
-            x = turns - ((turns + magic) - magic)
+    near = near_ref.shape[1]
+    per_block = (beams - near) // blocks
+
+    def fill(target, first, origin, count):
+        for step in range(count // rows):
+            turns = jnp.dot(
+                dirs[pl.ds(origin + first + step * rows, rows), :],
+                places,
+                preferred_element_type=jnp.float32,
+            )
+            x = turns - jnp.round(turns)
             square = x * x
             s = x * horner(sine_c, square)
             c = horner(cosine_c, square)
-            phase_ref[0, at, :] = 1.0 - s * s
-            phase_ref[1, at, :] = s * c
+            at = pl.ds(first + step * rows, rows)
+            target[0, at, :] = 1.0 - s * s
+            target[1, at, :] = s * c
+
+    for block in range(blocks):
+        fill(far_ref, block * per_block, near, per_block)
         part = pl.ds(block * per_block, per_block)
-        outgoing.append(start(phase_ref.at[:, part], phase_hbm.at[:, part], out_sems.at[block]))
-
+        outgoing.append(start(far_ref.at[:, part], far_hbm.at[:, part], out_sems.at[block]))
+    fill(near_ref, 0, 0, near)
     for copy in outgoing:
         copy.wait()
 
@@ -223,34 +236,35 @@
     beams = pointing.shape[1]
     stations = positions.shape[1]
     samples = volts.shape[1]
-    blocks = 8
-    phase = (2, beams, stations)
+    blocks = 4
+    near = beams * NEAR // 8
+    far = (2, beams - near, stations)
     rhs = (2, 2 * stations, samples)
     return pl.pallas_call(
         functools.partial(phasor_kernel, 64, blocks, total),
         out_shape=(
-            jax.ShapeDtypeStruct(phase, jnp.float32),
+            jax.ShapeDtypeStruct((2, near, stations), jnp.float32),
+            pltpu.HBM(far, jnp.float32),
             jax.ShapeDtypeStruct(rhs, jnp.bfloat16),
         ),
         in_specs=[HBM_SPEC] * 4,
-        out_specs=(HBM_SPEC, HBM_SPEC),
+        out_specs=(VMEM_SPEC, HBM_SPEC, VMEM_SPEC),
         scratch_shapes=[
             pltpu.VMEM(volts.shape, volts.dtype),
             pltpu.VMEM(positions.shape, jnp.float32),
             pltpu.VMEM(directions.shape, jnp.float32),
             pltpu.VMEM(pointing.shape, jnp.int32),
-            pltpu.VMEM(phase, jnp.float32),
-            pltpu.VMEM(rhs, jnp.bfloat16),
+            pltpu.VMEM(far, jnp.float32),
             pltpu.VMEM((beams, 32), jnp.bfloat16),
             pltpu.SemaphoreType.DMA((4,)),
-            pltpu.SemaphoreType.DMA((blocks + 2,)),
+            pltpu.SemaphoreType.DMA((blocks,)),
         ],
-        compiler_params=pltpu.CompilerParams(vmem_limit_bytes=GRANT - 2 * MIB),
+        compiler_params=pltpu.CompilerParams(vmem_limit_bytes=GRANT - 24 * MIB),
         cost_estimate=pl.CostEstimate(
             flops=60 * beams * stations, bytes_accessed=8 * MIB, transcendentals=0
         ),
         name="phasors",
-    )(volts, positions, directions, pointing)
+    )(*map(in_hbm, (volts, positions, directions, pointing)))
 
 
 def invert_small(left):
@@ -338,36 +352,23 @@
 
 
 def beam_kernel(
-    sizes, splits, cal_ref, phase_hbm, rhs_hbm, out_ref, fitted_ref,
-    phase_ref, rhs_ref, target, keep, lean, history, sems,
+    cal_ref, near_ref, far_hbm, rhs_ref, out_ref, fitted_ref,
+    far_ref, target, keep, lean, history, sems,
 ):
-    stations = phase_ref.shape[2]
-    beams = phase_ref.shape[1]
+    near, stations = near_ref.shape[1:]
     half = rhs_ref.shape[2] // 2
-    edges = [sum(sizes[:block]) * beams // sum(sizes) for block in range(len(sizes) + 1)]
-
-    def fetch(block):
-        part = pl.ds(edges[block], edges[block + 1] - edges[block])
-        return start(phase_hbm.at[:, part], phase_ref.at[:, part], sems.at[2 + block])
-
-    copies = [fetch(0)]
-    rhs_copies = [start(rhs_hbm.at[p], rhs_ref.at[p], sems.at[p]) for p in range(2)]
-    copies += [fetch(later) for later in range(1, min(2, len(sizes)))]
+    far_copy = start(far_hbm, far_ref, sems.at[0])
     fitted = solve(cal_ref, target, keep, lean, history)
     fitted_ref[:, : stations // 2] = fitted[0:4]
     fitted_ref[:, stations // 2 :] = fitted[4:8]
     _, own = unpack(cal_ref[lax.axis_index("chan")])
     dense = fitted * jnp.where(own > 0.0, stations ** (-0.5), 0.0)
     gains = jnp.concatenate([dense[0:4], dense[4:8]], 1)
-    for copy in rhs_copies:
-        copy.wait()
-    for group in range(len(sizes)):
-        copies[group].wait()
-        if group == 0:
-            copies += [fetch(later) for later in range(2, len(sizes))]
-        rows = (edges[group + 1] - edges[group]) // splits[group]
-        for block in range(splits[group]):
-            part = pl.ds(edges[group] + block * rows, rows)
+
+    def detect(phase_ref, origin, splits):
+        rows = phase_ref.shape[1] // splits
+        for block in range(splits):
+            part = pl.ds(block * rows, rows)
             cosine = phase_ref[0, part]
             sine = phase_ref[1, part]
             power = None
@@ -375,40 +376,46 @@
                 re = gains[2 * polar : 2 * polar + 1]
                 im = gains[2 * polar + 1 : 2 * polar + 2]
                 w_re = (re * cosine - im * sine).astype(jnp.bfloat16)
-                w_im = (-(re * sine + im * cosine)).astype(jnp.bfloat16)
+                minus_im = (re * sine + im * cosine).astype(jnp.bfloat16)
                 lhs = jnp.concatenate(
-                    [jnp.concatenate([w_re, -w_im], 1), jnp.concatenate([w_im, w_re], 1)], 0
+                    [
+                        jnp.concatenate([w_re, minus_im], 1),
+                        jnp.concatenate([-minus_im, w_re], 1),
+                    ],
+                    0,
                 )
                 y = jnp.dot(lhs, rhs_ref[polar], preferred_element_type=jnp.float32)
                 y = y * y
                 y = y[:rows] + y[rows:]
                 power = y if power is None else power + y
-            out_ref[part, :] = ((power[:, :half] + power[:, half:]) * 0.5).astype(jnp.bfloat16)
-
-
-def fit_and_detect(cal, phase, rhs):
+            power = (power[:, :half] + power[:, half:]) * 0.5
+            out_ref[pl.ds(origin + block * rows, rows), :] = power.astype(jnp.bfloat16)
+
+    detect(near_ref, 0, SPLITS)
+    far_copy.wait()
+    detect(far_ref, near, SPLITS)
+
+
+def fit_and_detect(cal, near, far, rhs):
     total, _, half_stations = cal.shape
-    _, beams, stations = phase.shape
+    stations = near.shape[2]
+    beams = near.shape[1] + far.shape[1]
     samples = rhs.shape[2]
-    sizes, splits = (1, 3, 4), (1, 1, 1)
     state = pltpu.VMEM((total, 8, half_stations), jnp.float32)
     return pl.pallas_call(
-        functools.partial(beam_kernel, sizes, splits),
+        beam_kernel,
         out_shape=(
             jax.ShapeDtypeStruct((beams, samples // 2), jnp.bfloat16),
             jax.ShapeDtypeStruct((4, stations), jnp.float32),
         ),
-        in_specs=[VMEM_SPEC, HBM_SPEC, HBM_SPEC],
+        in_specs=[VMEM_SPEC, VMEM_SPEC, HBM_SPEC, VMEM_SPEC],
         out_specs=(VMEM_SPEC, VMEM_SPEC),
-        scratch_shapes=[
-            pltpu.VMEM(phase.shape, jnp.float32),
-            pltpu.VMEM(rhs.shape, jnp.bfloat16),
-        ]
+        scratch_shapes=[pltpu.VMEM(far.shape, jnp.float32)]
         + [state] * 4
-        + [pltpu.SemaphoreType.DMA((2 + len(sizes),))],
-        compiler_params=pltpu.CompilerParams(vmem_limit_bytes=GRANT - 11 * MIB),
+        + [pltpu.SemaphoreType.DMA((1,))],
+        compiler_params=pltpu.CompilerParams(vmem_limit_bytes=GRANT - 24 * MIB),
         name="beams",
-    )(cal, phase, rhs)
+    )(cal, near, in_hbm(far), rhs)
 
 
 def body(voltages, cal_num, cal_weight, flags, positions, directions, pointing):
@@ -417,8 +424,8 @@
     total = devices
     packed = pack(cal_num[0], cal_weight[0], flags, devices)
     cal = lax.all_to_all(packed, "chan", 0, 0, tiled=True)
-    phase, rhs = phasors(voltages[0], positions, directions, pointing[None, :], total)
-    power, fitted = fit_and_detect(cal, phase, rhs)
+    near, far, rhs = phasors(voltages[0], positions, directions, pointing[None, :], total)
+    power, fitted = fit_and_detect(cal, near, far, rhs)
     moved = lax.all_to_all(power, "chan", 0, 0, tiled=True)
     beams = power.shape[0] // devices
     beam_power = jnp.transpose(moved.reshape(devices, beams, power.shape[1]), (1, 0, 2))

time: 35.7 us -> 34.5 us (0.966)
  Pallas kernels: 10.4 us -> 8.18 us
  waiting for transfers between devices: 3.33 us -> 4.32 us
    pallas_call x1, Pallas kernels: 4.39 us -> 3.18 us  [fit_and_detect(): pl.pallas_call(beam_kernel, out_shape=(jax.ShapeDtypeStruct((beams, sampl...]
    all_to_all x1, waiting for transfers between devices: 3.33 us -> 4.32 us  [body(): cal = lax.all_to_all(packed, 'chan', 0, 0, tiled=True)]
    pallas_call x1, Pallas kernels: 4.56 us -> 3.57 us  [phasors(): pl.pallas_call(functools.partial(phasor_kernel, 64, blocks, total), out_s...]
  transfers between devices with their start and end apart: 1 -> 1, of which waited for: 1 -> 1; matrix products, arithmetic and copies ran while one was open for 0% -> 0% of each run, Pallas kernels for 13% -> 10%
where the time goes in v6:
time: 34.5 us; the launch traced here: 34.1 us
  blocking collectives  12.6 us (37%)
  Pallas kernels  8.18 us (24%)
  starting transfers between devices  7.43 us (22%)
  waiting for transfers between devices  4.32 us (13%)
  local copies, waits for them, and re-layouts  0.88 us (3%)
  between operations  0.66 us (2%)
    all_to_all x1, blocking collectives, body(): moved = lax.all_to_all(power, 'chan', 0, 0, tiled=True)  12.6 us
    all_to_all x1, starting transfers between devices, body(): cal = lax.all_to_all(packed, 'chan', 0, 0, tiled=True)  7.43 us
    all_to_all x1, waiting for transfers between devices, body(): cal = lax.all_to_all(packed, 'chan', 0, 0, tiled=True)  4.32 us
    pallas_call x1, Pallas kernels, phasors(): pl.pallas_call(functools.partial(phasor_kernel, 64, blocks, total), out_s...  3.57 us
    pallas_call x1, Pallas kernels, fit_and_detect(): pl.pallas_call(beam_kernel, out_shape=(jax.ShapeDtypeStruct((beams, sampl...  3.18 us
    pallas_call x1, Pallas kernels, pack(): pl.pallas_call(pack_kernel, out_shape=jax.ShapeDtypeStruct((devices, 16,...  1.43 us
    unnamed x1, local copies, waits for them, and re-layouts  0.88 us
  transfers between devices with their start and end apart: 1, of which 1 were waited for; matrix products, arithmetic and copies ran while one was open for 0% of the time, Pallas kernels for 10%

profile of v6, /device:TPU:0, one launch (start us, length us, event | category | flops | bytes accessed | tf_op | source)
XLA Modules:
  0.0 34.1 jit_solution(10915251726980551401)
XLA Ops:
  0.6 1.4 %pack.1 = s16[16,16,256]{2,1,0:T(8,128)(2,1)} custom-call(f32[4,512]{1,0:T(4,128)} %bitcast.10, f32[2,512]{1,0:T(2,128)} %bitcast.12, s32[1,512]{1,0:T(1,128)} %flag_hbm.1), custom_call_target="tpu_custom_call" | custom-call | tf_op jit(solution)/shard_map/pack/pallas_call | solution.py:112
  2.1 7.4 %all-to-all-start = ((s16[16,16,256]{2,1,0:T(8,128)(2,1)}), s16[16,16,256]{2,1,0:T(8,128)(2,1)S(1)}, u32[]{:S(2)}, u32[]{:S(2)}) async-start(s16[16,16,256]{2,1,0:T(8,128)(2,1)} %pack.1), calls=%async_computation | async-start | bytes 262144 | tf_op jit(solution)/shard_map/all_to_all | solution.py:426
  9.5 3.6 %phasors.1 = (f32[2,512,512]{2,1,0:T(8,128)S(1)}, f32[2,512,512]{2,1,0:T(8,128)}, bf16[2,1024,256]{2,1,0:T(8,128)(2,1)S(1)}) custom-call(bf16[2,256,1024]{2,1,0:T(8,128)(2,1)} %bitcast.8, f32[2,512]{1,0:T(2,128)} %pos_hbm.1, f32[2,1024]{1,0:T(2,128)} %dir_hbm.1, s32[1,1024]{1,0:T(1,128)} %bitcast.11), custom_call_target="tpu_custom_call" | custom-call | flops 31457280 | bytes 8388608 | tf_op jit(solution)/shard_map/phasors/pallas_call | solution.py:243
  13.1 4.3 %all-to-all-done.cal_ref = s16[16,16,256]{2,1,0:T(8,128)(2,1)S(1)} async-done(((s16[16,16,256]{2,1,0:T(8,128)(2,1)}), s16[16,16,256]{2,1,0:T(8,128)(2,1)S(1)}, u32[]{:S(2)}, u32[]{:S(2)}) %all-to-all-start) | async-done | bytes 131104 | tf_op jit(solution)/shard_map/all_to_all | solution.py:426
  17.4 3.2 %beams.1 = (bf16[1024,128]{1,0:T(8,128)(2,1)S(1)}, f32[4,512]{1,0:T(4,128)}) custom-call(s16[16,16,256]{2,1,0:T(8,128)(2,1)S(1)} %all-to-all-done.cal_ref, f32[2,512,512]{2,1,0:T(8,128)S(1)} %get-tuple-element.7.near_ref, f32[2,512,512]{2,1,0:T(8,128)} %get-tuple-element.8.far_hbm, bf16[2,1024,256]{2,1,0:T(8,128)(2,1)S(1)} %get-tuple-element.9.rhs_ref), custom_call_target="tpu_custom_call" | custom-call | tf_op jit(solution)/shard_map/beams/pallas_call | solution.py:405
  20.6 12.6 %all_to_all.14 = bf16[16,64,128]{2,1,0:T(8,128)(2,1)S(1)} all-to-all(bf16[16,64,128]{2,1,0:T(8,128)(2,1)S(1)} %bitcast.7), channel_id=1, replica_groups=mesh['group'=2,'chan'=16] {'chan'}, dimensions={0} | all-to-all | bytes 524288 | tf_op jit(solution)/shard_map/all_to_all | solution.py:429
  33.2 0.9 %copy.10 = bf16[64,16,128]{2,1,0:T(8,128)(2,1)} copy(bf16[64,16,128]{2,0,1:T(8,128)(2,1)S(1)} %bitcast.9) | data formatting | bytes 524288
Async XLA Ops:
  2.1 15.3 %all-to-all-start = ((s16[16,16,256]{2,1,0:T(8,128)(2,1)}), s16[16,16,256]{2,1,0:T(8,128)(2,1)S(1)}, u32[]{:S(2)}, u32[]{:S(2)}) async-start(s16[16,16,256]{2,1,0:T(8,128)(2,1)} %pack.1), calls=%async_computation | async-start | bytes 262144 | tf_op jit(solution)/shard_map/all_to_all | solution.py:426

commit v7 on v6

--- a/solution.py
+++ b/solution.py
@@ -418,6 +418,22 @@
     )(cal, near, in_hbm(far), rhs)
 
 
+def arrange_kernel(moved_ref, out_ref):
+    out_ref[...] = jnp.swapaxes(moved_ref[...], 0, 1)
+
+
+def arrange(moved):
+    channels, beams, samples = moved.shape
+    return pl.pallas_call(
+        arrange_kernel,
+        out_shape=jax.ShapeDtypeStruct((beams, channels, samples), moved.dtype),
+        in_specs=[VMEM_SPEC],
+        out_specs=VMEM_SPEC,
+        compiler_params=pltpu.CompilerParams(vmem_limit_bytes=GRANT - 24 * MIB),
+        name="arrange",
+    )(moved)
+
+
 def body(voltages, cal_num, cal_weight, flags, positions, directions, pointing):
     devices = lax.axis_size("chan")
     assert voltages.shape[0] == 1
@@ -427,8 +443,7 @@
     near, far, rhs = phasors(voltages[0], positions, directions, pointing[None, :], total)
     power, fitted = fit_and_detect(cal, near, far, rhs)
     moved = lax.all_to_all(power, "chan", 0, 0, tiled=True)
-    beams = power.shape[0] // devices
-    beam_power = jnp.transpose(moved.reshape(devices, beams, power.shape[1]), (1, 0, 2))
+    beam_power = arrange(moved.reshape(devices, power.shape[0] // devices, power.shape[1]))
     return beam_power, fitted[None]
 
 

time: 34.5 us -> 34.4 us (level)
  local copies, waits for them, and re-layouts: 0.88 us -> 0 us
  Pallas kernels: 8.18 us -> 8.94 us
    unnamed x1 -> x0, local copies, waits for them, and re-layouts: 0.88 us -> none
    pallas_call x0 -> x1, Pallas kernels: none -> 0.76 us  [arrange(): pl.pallas_call(arrange_kernel, out_shape=jax.ShapeDtypeStruct((beams, cha...]
where the time goes in v7:
time: 34.4 us; the launch traced here: 34 us
  blocking collectives  12.6 us (37%)
  Pallas kernels  8.94 us (26%)
  starting transfers between devices  7.43 us (22%)
  waiting for transfers between devices  4.32 us (13%)
  between operations  0.66 us (2%)
    all_to_all x1, blocking collectives, body(): moved = lax.all_to_all(power, 'chan', 0, 0, tiled=True)  12.6 us
    all_to_all x1, starting transfers between devices, body(): cal = lax.all_to_all(packed, 'chan', 0, 0, tiled=True)  7.43 us
    all_to_all x1, waiting for transfers between devices, body(): cal = lax.all_to_all(packed, 'chan', 0, 0, tiled=True)  4.32 us
    pallas_call x1, Pallas kernels, phasors(): pl.pallas_call(functools.partial(phasor_kernel, 64, blocks, total), out_s...  3.57 us
    pallas_call x1, Pallas kernels, fit_and_detect(): pl.pallas_call(beam_kernel, out_shape=(jax.ShapeDtypeStruct((beams, sampl...  3.18 us
    pallas_call x1, Pallas kernels, pack(): pl.pallas_call(pack_kernel, out_shape=jax.ShapeDtypeStruct((devices, 16,...  1.43 us
    pallas_call x1, Pallas kernels, arrange(): pl.pallas_call(arrange_kernel, out_shape=jax.ShapeDtypeStruct((beams, cha...  0.76 us
  transfers between devices with their start and end apart: 1, of which 1 were waited for; matrix products, arithmetic and copies ran while one was open for 0% of the time, Pallas kernels for 10%

profile of v7, /device:TPU:0, one launch (start us, length us, event | category | flops | bytes accessed | tf_op | source)
XLA Modules:
  0.0 34.0 jit_solution(6144518102612650492)
XLA Ops:
  0.6 1.4 %pack.1 = s16[16,16,256]{2,1,0:T(8,128)(2,1)} custom-call(f32[4,512]{1,0:T(4,128)} %bitcast.8, f32[2,512]{1,0:T(2,128)} %bitcast.10, s32[1,512]{1,0:T(1,128)} %flag_hbm.1), custom_call_target="tpu_custom_call" | custom-call | tf_op jit(solution)/shard_map/pack/pallas_call | solution.py:112
  2.1 7.4 %all-to-all-start = ((s16[16,16,256]{2,1,0:T(8,128)(2,1)}), s16[16,16,256]{2,1,0:T(8,128)(2,1)S(1)}, u32[]{:S(2)}, u32[]{:S(2)}) async-start(s16[16,16,256]{2,1,0:T(8,128)(2,1)} %pack.1), calls=%async_computation | async-start | bytes 262144 | tf_op jit(solution)/shard_map/all_to_all | solution.py:442
  9.5 3.6 %phasors.1 = (f32[2,512,512]{2,1,0:T(8,128)S(1)}, f32[2,512,512]{2,1,0:T(8,128)}, bf16[2,1024,256]{2,1,0:T(8,128)(2,1)S(1)}) custom-call(bf16[2,256,1024]{2,1,0:T(8,128)(2,1)} %bitcast.7, f32[2,512]{1,0:T(2,128)} %pos_hbm.1, f32[2,1024]{1,0:T(2,128)} %dir_hbm.1, s32[1,1024]{1,0:T(1,128)} %bitcast.9), custom_call_target="tpu_custom_call" | custom-call | flops 31457280 | bytes 8388608 | tf_op jit(solution)/shard_map/phasors/pallas_call | solution.py:243
  13.1 4.3 %all-to-all-done.cal_ref = s16[16,16,256]{2,1,0:T(8,128)(2,1)S(1)} async-done(((s16[16,16,256]{2,1,0:T(8,128)(2,1)}), s16[16,16,256]{2,1,0:T(8,128)(2,1)S(1)}, u32[]{:S(2)}, u32[]{:S(2)}) %all-to-all-start) | async-done | bytes 131104 | tf_op jit(solution)/shard_map/all_to_all | solution.py:442
  17.4 3.2 %beams.1 = (bf16[1024,128]{1,0:T(8,128)(2,1)S(1)}, f32[4,512]{1,0:T(4,128)}) custom-call(s16[16,16,256]{2,1,0:T(8,128)(2,1)S(1)} %all-to-all-done.cal_ref, f32[2,512,512]{2,1,0:T(8,128)S(1)} %get-tuple-element.7.near_ref, f32[2,512,512]{2,1,0:T(8,128)} %get-tuple-element.8.far_hbm, bf16[2,1024,256]{2,1,0:T(8,128)(2,1)S(1)} %get-tuple-element.9.rhs_ref), custom_call_target="tpu_custom_call" | custom-call | tf_op jit(solution)/shard_map/beams/pallas_call | solution.py:405
  20.6 12.6 %all_to_all.14.moved_ref = bf16[16,64,128]{2,1,0:T(8,128)(2,1)S(1)} all-to-all(bf16[16,64,128]{2,1,0:T(8,128)(2,1)S(1)} %bitcast.6), channel_id=1, replica_groups=mesh['group'=2,'chan'=16] {'chan'}, dimensions={0} | all-to-all | bytes 524288 | tf_op jit(solution)/shard_map/all_to_all | solution.py:445
  33.2 0.8 %arrange.1 = bf16[64,16,128]{2,1,0:T(8,128)(2,1)} custom-call(bf16[16,64,128]{2,1,0:T(8,128)(2,1)S(1)} %all_to_all.14.moved_ref), custom_call_target="tpu_custom_call" | custom-call | tf_op jit(solution)/shard_map/arrange/pallas_call | solution.py:427
Async XLA Ops:
  2.1 15.3 %all-to-all-start = ((s16[16,16,256]{2,1,0:T(8,128)(2,1)}), s16[16,16,256]{2,1,0:T(8,128)(2,1)S(1)}, u32[]{:S(2)}, u32[]{:S(2)}) async-start(s16[16,16,256]{2,1,0:T(8,128)(2,1)} %pack.1), calls=%async_computation | async-start | bytes 262144 | tf_op jit(solution)/shard_map/all_to_all | solution.py:442
